TPU v7x, 512 devices: a whole 4x8x8 slice. The times are simulated.
512 devices in a mesh: fsdp: 16 (over y, core), ctx: 32 (over z, x).
Axes of the slice: x: 4, y: 8, z: 8, core: 2. Of those that a mesh axis runs over, the one named last changes fastest.
Arguments:
- featurized: bfloat16 [4096, 3, 4096], P('ctx', None, 'fsdp'), may hold values from -6 to 6
- short_taps: float32 [3, 3, 4096], P(None, None, 'fsdp'), may hold values from -3 to 3
- residues: float32 [4096, 16], P('fsdp'), may hold values from -1.5 to 1.5
- decay_rates: float32 [4096, 16], P('fsdp'), may hold values from 0.00012207031 to 0.05
- w_out: bfloat16 [4096, 8192], P('fsdp', 'ctx'), may hold values from -0.09375 to 0.09375
- grad_out: bfloat16 [4096, 8192], P('ctx'), may hold values from -6 to 6
Outputs:
- block_output: bfloat16 [4096, 8192], P('ctx', 'fsdp')
- grad_features: bfloat16 [4096, 3, 4096], P('ctx', None, 'fsdp')
All inputs are finite; a program needn't handle non-finite values.
Results may differ from a plain program's by a relative error of at most 0.02.
Values may be sent and summed in bfloat16 or wider, within the bound.
A program may use at most 64 MiB of HBM per device.

v0:
```python
import math

import jax
import jax.numpy as jnp
from jax import lax
from jax.sharding import PartitionSpec as P

HIGHEST = lax.Precision.HIGHEST


def swapped(block, axis, distance):
    count = lax.axis_size(axis)
    route = []
    for low in range(count):
        high = low | 1 << distance
        if high != low and high < count:
            route += [(low, high), (high, low)]
    return lax.ppermute(block, axis, route)


def shifted(block, axis, distance):
    devices = range(lax.axis_size(axis))
    route = [(i - distance, i) for i in devices if i - distance in devices]
    return lax.ppermute(block, axis, route)


def angles(product_index, modulus):
    phases = (product_index % modulus).astype(jnp.float32) * (2.0 * math.pi / modulus)
    return (jnp.cos(phases), jnp.sin(phases))


def complex_contract(pattern, table_re, table_im, real_part, imag_part):
    first_term = jnp.einsum(pattern, table_re, real_part, precision=HIGHEST)
    second_term = jnp.einsum(pattern, table_im, imag_part, precision=HIGHEST)
    third_term = jnp.einsum(pattern, table_re, imag_part, precision=HIGHEST)
    fourth_term = jnp.einsum(pattern, table_im, real_part, precision=HIGHEST)
    return (first_term - second_term, third_term + fourth_term)


def token_tables(tokens_here):
    positions_all = jnp.arange(tokens_here)
    return angles(positions_all[:, None] * positions_all[None, :], tokens_here)


def reversed_bits(my_rank, bit_count):
    result = jnp.zeros((), jnp.int32)
    for section_bit in range(bit_count):
        result = result + (my_rank >> section_bit & 1) * (1 << bit_count - 1 - section_bit)
    return result


def partner_step(values_now, section_bit, my_rank, inverse):
    partner_data = swapped(values_now.astype(jnp.bfloat16), "ctx", section_bit).astype(
        values_now.dtype
    )
    half_span = 1 << section_bit
    upper_side = my_rank >> section_bit & 1 == 1
    cos_turn, sin_turn = angles(my_rank % half_span, 2 * half_span)
    if inverse:
        spun_re = partner_data[0] * cos_turn - partner_data[1] * sin_turn
        spun_im = partner_data[1] * cos_turn + partner_data[0] * sin_turn
        lower_new = jnp.stack([values_now[0] + spun_re, values_now[1] + spun_im]) * 0.5
        mine_re = values_now[0] * cos_turn - values_now[1] * sin_turn
        mine_im = values_now[1] * cos_turn + values_now[0] * sin_turn
        upper_new = jnp.stack([partner_data[0] - mine_re, partner_data[1] - mine_im]) * 0.5
    else:
        lower_new = values_now + partner_data
        differ = partner_data - values_now
        upper_new = jnp.stack(
            [
                differ[0] * cos_turn + differ[1] * sin_turn,
                differ[1] * cos_turn - differ[0] * sin_turn,
            ]
        )
    return jnp.where(upper_side, upper_new, lower_new)


def forward_partners(signal):
    tokens_here = signal.shape[0]
    devices = lax.axis_size("ctx")
    bit_count = devices.bit_length() - 1
    my_rank = lax.axis_index("ctx")
    full_length = 2 * devices * tokens_here
    half_turn = my_rank.astype(jnp.float32) * (math.pi / devices)
    values_now = jnp.stack(
        [
            jnp.stack([signal, signal * jnp.cos(half_turn)]),
            jnp.stack([jnp.zeros_like(signal), -signal * jnp.sin(half_turn)]),
        ]
    )
    for section_bit in reversed(range(bit_count)):
        values_now = partner_step(values_now, section_bit, my_rank, False)
    spectral_rows = 2 * reversed_bits(my_rank, bit_count) + jnp.arange(2)
    cos_twist, sin_twist = angles(
        spectral_rows[:, None] * jnp.arange(tokens_here)[None, :], full_length
    )
    cos_twist = cos_twist[:, :, None, None]
    sin_twist = sin_twist[:, :, None, None]
    twist_re = values_now[0] * cos_twist + values_now[1] * sin_twist
    twist_im = values_now[1] * cos_twist - values_now[0] * sin_twist
    cos_tokens, sin_tokens = token_tables(tokens_here)
    return complex_contract("ks,esgc->ekgc", cos_tokens, -sin_tokens, twist_re, twist_im)


def inverse_partners(spec_re, spec_im):
    tokens_here = spec_re.shape[1]
    devices = lax.axis_size("ctx")
    bit_count = devices.bit_length() - 1
    my_rank = lax.axis_index("ctx")
    full_length = 2 * devices * tokens_here
    cos_tokens, sin_tokens = token_tables(tokens_here)
    plain_re, plain_im = complex_contract("sk,ekgc->esgc", cos_tokens, sin_tokens, spec_re, spec_im)
    spectral_rows = 2 * reversed_bits(my_rank, bit_count) + jnp.arange(2)
    cos_twist, sin_twist = angles(
        spectral_rows[:, None] * jnp.arange(tokens_here)[None, :], full_length
    )
    cos_twist = cos_twist[:, :, None, None]
    sin_twist = sin_twist[:, :, None, None]
    twist_re = plain_re * cos_twist - plain_im * sin_twist
    twist_im = plain_re * sin_twist + plain_im * cos_twist
    values_now = jnp.stack([twist_re, twist_im])
    for section_bit in range(bit_count):
        values_now = partner_step(values_now, section_bit, my_rank, True)
    half_turn = my_rank.astype(jnp.float32) * (math.pi / devices)
    real_part = (
        values_now[0, 0]
        + values_now[0, 1] * jnp.cos(half_turn)
        - values_now[1, 1] * jnp.sin(half_turn)
    )
    return real_part / (2.0 * tokens_here)


def to_spectrum(signal):
    return forward_partners(signal)


def from_spectrum(spec_re, spec_im):
    return inverse_partners(spec_re, spec_im)


def modal_spectrum(residues, decay_rates, spectral_rows, tokens_here, devices):
    full_length = 2 * devices * tokens_here
    sequence = devices * tokens_here
    frequency = spectral_rows[:, None] + 2 * devices * jnp.arange(tokens_here)[None, :]
    angle_now = frequency.astype(jnp.float32) * (math.pi / full_length)
    half_sine = jnp.sin(angle_now)[:, :, None]
    full_sine = jnp.sin(2.0 * angle_now)[:, :, None]
    parity_sign = (1 - 2 * (spectral_rows % 2)).astype(jnp.float32)[:, None, None]

    def add_mode(mode_index, totals):
        rates_now = lax.dynamic_slice_in_dim(decay_rates, mode_index, 1, 1)[:, 0]
        weight = lax.dynamic_slice_in_dim(residues, mode_index, 1, 1)[:, 0] * jnp.sqrt(rates_now)
        decay_now = jnp.exp(-rates_now)
        numerator = 1.0 - parity_sign * jnp.exp(-rates_now * sequence)
        denom_re = -jnp.expm1(-rates_now) + 2.0 * decay_now * half_sine * half_sine
        denom_im = decay_now * full_sine
        scaled = weight * numerator / (denom_re * denom_re + denom_im * denom_im)
        return (totals[0] + scaled * denom_re, totals[1] - scaled * denom_im)

    empty = jnp.zeros((spectral_rows.shape[0], tokens_here, residues.shape[0]), jnp.float32)
    spec_re, spec_im = lax.fori_loop(0, residues.shape[1], add_mode, (empty, empty))
    return (spec_re[:, :, None, :], spec_im[:, :, None, :])


def own_filter(residues, decay_rates, tokens_here):
    devices = lax.axis_size("ctx")
    my_rank = lax.axis_index("ctx")
    pair_rank = reversed_bits(my_rank, devices.bit_length() - 1)
    return modal_spectrum(
        residues, decay_rates, 2 * pair_rank + jnp.arange(2), tokens_here, devices
    )


def per_device(featurized, short_taps, residues, decay_rates, w_out, grad_out):
    tokens_here = featurized.shape[0]
    before = shifted(featurized[tokens_here - 2 :], "ctx", 1)
    raw_values = featurized.astype(jnp.float32)
    extended = jnp.concatenate([before.astype(jnp.float32), raw_values], axis=0)
    mixed_in = (
        short_taps[0] * extended[2:]
        + short_taps[1] * extended[1 : tokens_here + 1]
        + short_taps[2] * extended[:tokens_here]
    )
    query_part = mixed_in[:, 0]
    key_part = mixed_in[:, 1]
    value_part = mixed_in[:, 2]
    carried = key_part * value_part
    signal_re, signal_im = to_spectrum(carried[:, None, :])
    filter_re, filter_im = own_filter(residues, decay_rates, tokens_here)
    conv_re = signal_re * filter_re - signal_im * filter_im
    conv_im = signal_re * filter_im + signal_im * filter_re
    convolved = from_spectrum(conv_re, conv_im)[:, 0]
    gated_out = (query_part * convolved).astype(jnp.bfloat16)
    w_full = lax.all_gather(w_out, "ctx", axis=1, tiled=True)
    partial_sum = jnp.dot(gated_out, w_full, preferred_element_type=jnp.float32)
    block_output = lax.psum_scatter(
        partial_sum.astype(jnp.bfloat16), "fsdp", scatter_dimension=1, tiled=True
    )
    grad_gated = lax.dot_general(
        grad_out, w_full, (((1,), (1,)), ((), ())), preferred_element_type=jnp.float32
    )
    grad_query = grad_gated * convolved
    grad_conv = grad_gated * query_part
    delta_re, delta_im = to_spectrum(grad_conv[:, None, :])
    back_re = filter_re * delta_re + filter_im * delta_im
    back_im = filter_re * delta_im - filter_im * delta_re
    grad_carried = from_spectrum(back_re, back_im)[:, 0]
    grad_mixed = jnp.stack([grad_query, grad_carried * value_part, grad_carried * key_part], axis=1)
    following = shifted(grad_mixed[:2], "ctx", -1)
    padded = jnp.concatenate([grad_mixed, following], axis=0)
    grad_features = (
        short_taps[0] * padded[:tokens_here]
        + short_taps[1] * padded[1 : tokens_here + 1]
        + short_taps[2] * padded[2:]
    ).astype(jnp.bfloat16)
    return (block_output, grad_features)


def solution(mesh):
    placed = (
        P("ctx", None, "fsdp"),
        P(None, None, "fsdp"),
        P("fsdp", None),
        P("fsdp", None),
        P("fsdp", "ctx"),
        P("ctx", None),
    )
    return jax.shard_map(
        per_device,
        mesh=mesh,
        in_specs=placed,
        out_specs=(P("ctx", "fsdp"), P("ctx", None, "fsdp")),
        check_vma=False,
    )
```

profile of v0, /device:TPU:1, one launch (start us, length us, event | category | flops | bytes accessed | tf_op | source)
XLA Modules:
  0.0 353.3 jit_solution(11547537968246586453)
XLA Ops:
  8.7 3.9 %collective-permute-start = (bf16[2,3,256]{2,0,1:T(2,128)(2,1)S(1)}, bf16[2,3,256]{2,0,1:T(2,128)(2,1)S(1)}, u32[]{:S(2)}, u32[]{:S(2)}) collective-permute-start(bf16[2,3,256]{2,0,1:T(2,128)(2,1)S(1)} %slice.158), channel_id=1, source_target_pairs={{0,1},{1,2},{2,3},{3,4},{4,5},{5,6},{6,7},{7,8},{8,9},{9,10},{10,1... | collective-permute-start | bytes 9224 | tf_op jit(solution)/shard_map/ppermute | solution.py:24
  13.9 1.0 convert_element_type.334
  16.0 12.7 %collective-permute-start.1 = (bf16[2,2,128,1,256]{4,2,1,3,0:T(8,128)(2,1)}, bf16[2,2,128,1,256]{4,2,1,3,0:T(8,128)(2,1)}, u32[]{:S(2)}, u32[]{:S(2)}) collective-permute-start(bf16[2,2,128,1,256]{4,2,1,3,0:T(8,128)(2,1)} %fusion.53), channel_id=1, source_target_pairs={{0,16},{16,0},{1,17},{17,1},{2,18},{18,2},{3,19},{19,3},{4,20},{20... | collective-permute-start | bytes 786440 | tf_op jit(solution)/shard_map/ppermute | solution.py:18
  28.7 78.4 %all-gather.2.cloned.1.call-done = bf16[256,8192]{1,0:T(8,128)(2,1)} async-done(((bf16[256,256]{1,0:T(8,128)(2,1)}), bf16[256,8192]{1,0:T(8,128)(2,1)}) %all-gather.2.cloned.1.call-update) | async-done | bytes 4194320 | tf_op jit(solution)/shard_map/all_gather | solution.py:194
  107.2 3.7 %fusion.254 = f32[128,256]{1,0:T(8,128)S(1)} fusion(bf16[128,8192]{1,0:T(8,128)(2,1)S(1)} %copy-done, bf16[256,8192]{1,0:T(8,128)(2,1)} %all-gather.2.cloned.1.call-done), kind=kOutput, calls=%fused_computation.407 | convolution fusion | flops 536870912 | bytes 6422528 | tf_op jit(solution)/shard_map/dot_general | solution.py:199
  111.6 4.2 %collective-permute-start.11 = (bf16[2,2,128,1,256]{4,2,1,3,0:T(8,128)(2,1)S(1)}, bf16[2,2,128,1,256]{4,2,1,3,0:T(8,128)(2,1)S(1)}, u32[]{:S(2)}, u32[]{:S(2)}) collective-permute-start(bf16[2,2,128,1,256]{4,2,1,3,0:T(8,128)(2,1)S(1)} %fusion.52), channel_id=1, source_target_pairs={{0,16},{16,0},{1,17},{17,1},{2,18},{18,2},{3,19},{19,3},{4,20},{20... | collective-permute-start | bytes 786440 | tf_op jit(solution)/shard_map/ppermute | solution.py:18
  115.9 29.6 %while.18 = (s32[]{:T(128)}, f32[2,128,256]{2,1,0:T(8,128)S(1)}, f32[2,128,256]{2,1,0:T(8,128)S(1)}, f32[256,16]{0,1:T(8,128)}, f32[256,16]{0,1:T(8,128)}, /*ind...) while((s32[]{:T(128)}, f32[2,128,256]{2,1,0:T(8,128)S(1)}, ...), condition=%wide.region_1.2_spmd.clone.clone.clone, body=%wide.region_0.1_spmd.clone.clone.clone.sunk | while | flops 921377 | bytes 1070735 | solution.py:161
  116.7 0.8 sine_bitcast_fusion.3
  118.6 0.8 sine_bitcast_fusion.3
  120.4 0.8 sine_bitcast_fusion.3
  122.3 0.8 sine_bitcast_fusion.3
  124.1 0.8 sine_bitcast_fusion.3
  126.0 0.8 sine_bitcast_fusion.3
  131.5 0.8 sine_bitcast_fusion.3
  135.2 0.8 sine_bitcast_fusion.3
  137.0 0.8 sine_bitcast_fusion.3
  140.7 0.8 sine_bitcast_fusion.3
  145.6 1.0 convert_subtract_fusion.9
  146.7 0.9 multiply_add_fusion.7
  147.7 1.7 fusion.248
  149.4 3.9 %collective-permute-start.2 = (bf16[2,2,128,1,256]{4,2,1,3,0:T(8,128)(2,1)}, bf16[2,2,128,1,256]{4,2,1,3,0:T(8,128)(2,1)S(1)}, u32[]{:S(2)}, u32[]{:S(2)}) collective-permute-start(bf16[2,2,128,1,256]{4,2,1,3,0:T(8,128)(2,1)} %get-tuple-element.293), channel_id=1, source_target_pairs={{0,8},{8,0},{1,9},{9,1},{2,10},{10,2},{3,11},{11,3},{4,12},{12,4},... | collective-permute-start | bytes 786440 | tf_op jit(solution)/shard_map/ppermute | solution.py:18
  154.2 1.1 fusion.232
  155.4 2.3 collective-permute-start.12
  157.7 8.9 %collective-permute-done.2 = bf16[2,2,128,1,256]{4,2,1,3,0:T(8,128)(2,1)S(1)} collective-permute-done((bf16[2,2,128,1,256]{4,2,1,3,0:T(8,128)(2,1)}, bf16[2,2,128,1,256]{4,2,1,3,0:T(8,128)(2,1)S(1)}, u32[]{:S(2)}, u32[]{:S(2)}) %collective-permute-start.2) | collective-permute-done | bytes 262176 | tf_op jit(solution)/shard_map/ppermute | solution.py:18
  166.8 1.9 collective-permute-start.3
  168.7 6.3 %collective-permute-done.12 = bf16[2,2,128,1,256]{4,2,1,3,0:T(8,128)(2,1)S(1)} collective-permute-done((bf16[2,2,128,1,256]{4,2,1,3,0:T(8,128)(2,1)S(1)}, bf16[2,2,128,1,256]{4,2,1,3,0:T(8,128)(2,1)S(1)}, u32[]{:S(2)}, u32[]{:S(2)}) %collective-permute-start.12) | collective-permute-done | bytes 262176 | tf_op jit(solution)/shard_map/ppermute | solution.py:18
  175.3 1.9 collective-permute-start.13
  177.2 3.2 collective-permute-done.3
  180.7 4.4 %collective-permute-start.4 = (bf16[2,2,128,1,256]{4,2,1,3,0:T(8,128)(2,1)S(1)}, bf16[2,2,128,1,256]{4,2,1,3,0:T(8,128)(2,1)S(1)}, u32[]{:S(2)}, u32[]{:S(2)}) collective-permute-start(bf16[2,2,128,1,256]{4,2,1,3,0:T(8,128)(2,1)S(1)} %get-tuple-element.289), channel_id=1, source_target_pairs={{0,2},{2,0},{1,3},{3,1},{4,6},{6,4},{5,7},{7,5},{8,10},{10,8},{9,1... | collective-permute-start | bytes 786440 | tf_op jit(solution)/shard_map/ppermute | solution.py:18
  185.1 0.9 collective-permute-done.13
  186.3 4.7 %collective-permute-start.14 = (bf16[2,2,128,1,256]{4,2,1,3,0:T(8,128)(2,1)S(1)}, bf16[2,2,128,1,256]{4,2,1,3,0:T(8,128)(2,1)S(1)}, u32[]{:S(2)}, u32[]{:S(2)}) collective-permute-start(bf16[2,2,128,1,256]{4,2,1,3,0:T(8,128)(2,1)S(1)} %get-tuple-element.269), channel_id=1, source_target_pairs={{0,2},{2,0},{1,3},{3,1},{4,6},{6,4},{5,7},{7,5},{8,10},{10,8},{9,1... | collective-permute-start | bytes 786440 | tf_op jit(solution)/shard_map/ppermute | solution.py:18
  191.3 1.9 collective-permute-start.5
  193.2 4.1 %collective-permute-done.14 = bf16[2,2,128,1,256]{4,2,1,3,0:T(8,128)(2,1)S(1)} collective-permute-done((bf16[2,2,128,1,256]{4,2,1,3,0:T(8,128)(2,1)S(1)}, bf16[2,2,128,1,256]{4,2,1,3,0:T(8,128)(2,1)S(1)}, u32[]{:S(2)}, u32[]{:S(2)}) %collective-permute-start.14) | collective-permute-done | bytes 262176 | tf_op jit(solution)/shard_map/ppermute | solution.py:18
  197.5 2.1 collective-permute-start.15
  199.6 2.8 collective-permute-done.5
  204.2 3.9 %collective-permute-done.15 = bf16[2,2,128,1,256]{4,2,1,3,0:T(8,128)(2,1)S(1)} collective-permute-done((bf16[2,2,128,1,256]{4,2,1,3,0:T(8,128)(2,1)S(1)}, bf16[2,2,128,1,256]{4,2,1,3,0:T(8,128)(2,1)S(1)}, u32[]{:S(2)}, u32[]{:S(2)}) %collective-permute-start.15) | collective-permute-done | bytes 262176 | tf_op jit(solution)/shard_map/ppermute | solution.py:18
  209.8 0.8 fusion.23
  210.6 0.8 fusion.22
  211.4 0.8 fusion.19
  212.1 0.8 fusion.82
  218.2 3.5 collective-permute-start.6
  221.7 3.7 %collective-permute-done.6 = bf16[2,2,128,1,256]{4,2,1,3,0:T(8,128)(2,1)S(1)} collective-permute-done((bf16[2,2,128,1,256]{4,2,1,3,0:T(8,128)(2,1)S(1)}, bf16[2,2,128,1,256]{4,2,1,3,0:T(8,128)(2,1)S(1)}, u32[]{:S(2)}, u32[]{:S(2)}) %collective-permute-start.6) | collective-permute-done | bytes 262176 | tf_op jit(solution)/shard_map/ppermute | solution.py:18
  225.7 1.9 collective-permute-start.7
  227.6 8.4 %collective-permute-done.7 = bf16[2,2,128,1,256]{4,2,1,3,0:T(8,128)(2,1)S(1)} collective-permute-done((bf16[2,2,128,1,256]{4,2,1,3,0:T(8,128)(2,1)S(1)}, bf16[2,2,128,1,256]{4,2,1,3,0:T(8,128)(2,1)S(1)}, u32[]{:S(2)}, u32[]{:S(2)}) %collective-permute-start.7) | collective-permute-done | bytes 262176 | tf_op jit(solution)/shard_map/ppermute | solution.py:18
  236.3 2.1 collective-permute-start.8
  238.5 5.0 %collective-permute-done.8 = bf16[2,2,128,1,256]{4,2,1,3,0:T(8,128)(2,1)S(1)} collective-permute-done((bf16[2,2,128,1,256]{4,2,1,3,0:T(8,128)(2,1)S(1)}, bf16[2,2,128,1,256]{4,2,1,3,0:T(8,128)(2,1)S(1)}, u32[]{:S(2)}, u32[]{:S(2)}) %collective-permute-start.8) | collective-permute-done | bytes 262176 | tf_op jit(solution)/shard_map/ppermute | solution.py:18
  243.7 2.2 collective-permute-start.9
  245.9 8.5 %collective-permute-done.9 = bf16[2,2,128,1,256]{4,2,1,3,0:T(8,128)(2,1)S(1)} collective-permute-done((bf16[2,2,128,1,256]{4,2,1,3,0:T(8,128)(2,1)S(1)}, bf16[2,2,128,1,256]{4,2,1,3,0:T(8,128)(2,1)S(1)}, u32[]{:S(2)}, u32[]{:S(2)}) %collective-permute-start.9) | collective-permute-done | bytes 262176 | tf_op jit(solution)/shard_map/ppermute | solution.py:18
  254.7 4.8 %collective-permute-start.10 = (bf16[2,2,128,1,256]{4,2,1,3,0:T(8,128)(2,1)S(1)}, bf16[2,2,128,1,256]{4,2,1,3,0:T(8,128)(2,1)S(1)}, u32[]{:S(2)}, u32[]{:S(2)}) collective-permute-start(bf16[2,2,128,1,256]{4,2,1,3,0:T(8,128)(2,1)S(1)} %get-tuple-element.275), channel_id=1, source_target_pairs={{0,16},{16,0},{1,17},{17,1},{2,18},{18,2},{3,19},{19,3},{4,20},{20... | collective-permute-start | bytes 786440 | tf_op jit(solution)/shard_map/ppermute | solution.py:18
  259.6 2.6 collective-permute-start.16
  262.2 4.3 %collective-permute-done.10 = bf16[2,2,128,1,256]{4,2,1,3,0:T(8,128)(2,1)S(1)} collective-permute-done((bf16[2,2,128,1,256]{4,2,1,3,0:T(8,128)(2,1)S(1)}, bf16[2,2,128,1,256]{4,2,1,3,0:T(8,128)(2,1)S(1)}, u32[]{:S(2)}, u32[]{:S(2)}) %collective-permute-start.10) | collective-permute-done | bytes 262176 | tf_op jit(solution)/shard_map/ppermute | solution.py:18
  266.8 2.0 convolution_convert_fusion
  269.2 6.3 %collective-permute-start.17 = (bf16[2,2,128,1,256]{4,2,1,3,0:T(8,128)(2,1)S(1)}, bf16[2,2,128,1,256]{4,2,1,3,0:T(8,128)(2,1)S(1)}, u32[]{:S(2)}, u32[]{:S(2)}) collective-permute-start(bf16[2,2,128,1,256]{4,2,1,3,0:T(8,128)(2,1)S(1)} %get-tuple-element.261), channel_id=1, source_target_pairs={{0,2},{2,0},{1,3},{3,1},{4,6},{6,4},{5,7},{7,5},{8,10},{10,8},{9,1... | collective-permute-start | bytes 786440 | tf_op jit(solution)/shard_map/ppermute | solution.py:18
  275.5 4.0 %collective-permute-done.17 = bf16[2,2,128,1,256]{4,2,1,3,0:T(8,128)(2,1)S(1)} collective-permute-done((bf16[2,2,128,1,256]{4,2,1,3,0:T(8,128)(2,1)S(1)}, bf16[2,2,128,1,256]{4,2,1,3,0:T(8,128)(2,1)S(1)}, u32[]{:S(2)}, u32[]{:S(2)}) %collective-permute-start.17) | collective-permute-done | bytes 262176 | tf_op jit(solution)/shard_map/ppermute | solution.py:18
  279.8 3.2 collective-permute-start.18
  283.0 3.9 %collective-permute-done.18 = bf16[2,2,128,1,256]{4,2,1,3,0:T(8,128)(2,1)S(1)} collective-permute-done((bf16[2,2,128,1,256]{4,2,1,3,0:T(8,128)(2,1)S(1)}, bf16[2,2,128,1,256]{4,2,1,3,0:T(8,128)(2,1)S(1)}, u32[]{:S(2)}, u32[]{:S(2)}) %collective-permute-start.18) | collective-permute-done | bytes 262176 | tf_op jit(solution)/shard_map/ppermute | solution.py:18
  287.2 4.8 %collective-permute-start.19 = (bf16[2,2,128,1,256]{4,2,1,3,0:T(8,128)(2,1)S(1)}, bf16[2,2,128,1,256]{4,2,1,3,0:T(8,128)(2,1)S(1)}, u32[]{:S(2)}, u32[]{:S(2)}) collective-permute-start(bf16[2,2,128,1,256]{4,2,1,3,0:T(8,128)(2,1)S(1)} %get-tuple-element.257), channel_id=1, source_target_pairs={{0,8},{8,0},{1,9},{9,1},{2,10},{10,2},{3,11},{11,3},{4,12},{12,4},... | collective-permute-start | bytes 786440 | tf_op jit(solution)/shard_map/ppermute | solution.py:18
  292.0 6.6 %collective-permute-done.19 = bf16[2,2,128,1,256]{4,2,1,3,0:T(8,128)(2,1)S(1)} collective-permute-done((bf16[2,2,128,1,256]{4,2,1,3,0:T(8,128)(2,1)S(1)}, bf16[2,2,128,1,256]{4,2,1,3,0:T(8,128)(2,1)S(1)}, u32[]{:S(2)}, u32[]{:S(2)}) %collective-permute-start.19) | collective-permute-done | bytes 262176 | tf_op jit(solution)/shard_map/ppermute | solution.py:18
  298.8 5.6 %collective-permute-start.20 = (bf16[2,2,128,1,256]{4,2,1,3,0:T(8,128)(2,1)S(1)}, bf16[2,2,128,1,256]{4,2,1,3,0:T(8,128)(2,1)S(1)}, u32[]{:S(2)}, u32[]{:S(2)}) collective-permute-start(bf16[2,2,128,1,256]{4,2,1,3,0:T(8,128)(2,1)S(1)} %get-tuple-element.255), channel_id=1, source_target_pairs={{0,16},{16,0},{1,17},{17,1},{2,18},{18,2},{3,19},{19,3},{4,20},{20... | collective-permute-start | bytes 786440 | tf_op jit(solution)/shard_map/ppermute | solution.py:18
  304.5 7.9 %collective-permute-done.20 = bf16[2,2,128,1,256]{4,2,1,3,0:T(8,128)(2,1)S(1)} collective-permute-done((bf16[2,2,128,1,256]{4,2,1,3,0:T(8,128)(2,1)S(1)}, bf16[2,2,128,1,256]{4,2,1,3,0:T(8,128)(2,1)S(1)}, u32[]{:S(2)}, u32[]{:S(2)}) %collective-permute-start.20) | collective-permute-done | bytes 262176 | tf_op jit(solution)/shard_map/ppermute | solution.py:18
  312.8 1.3 collective-permute-start.21
  314.1 3.4 collective-permute-done.21
  317.5 0.8 fusion.49
  318.3 28.2 %reduce-scatter.2.cloned.1.call-done = bf16[128,512]{1,0:T(8,128)(2,1)} async-done(((bf16[128,8192]{1,0:T(8,128)(2,1)}), bf16[128,512]{1,0:T(8,128)(2,1)}) %reduce-scatter.2.cloned.1.call-update) | async-done | bytes 131088 | tf_op jit(solution)/shard_map/reduce_scatter | solution.py:196
  (199 shorter events, 38.9 us)
Async XLA Ops:
  7.2 100.0 %copy-start = (bf16[128,8192]{1,0:T(8,128)(2,1)S(1)}, bf16[128,8192]{1,0:T(8,128)(2,1)}, u32[]{:S(2)}) copy-start(bf16[128,8192]{1,0:T(8,128)(2,1)} %param.13) | copy-start | bytes 6291460
  7.2 100.0 %all-gather.2.cloned.1.call-start = ((), (), s32[]{:S(2)}) async-start(), calls=%async_computation.1 | async-start | bytes 4325376 | tf_op jit(solution)/shard_map/all_gather | solution.py:194
  7.9 338.6 %reduce-scatter.2.cloned.1.call-start = ((), (), s32[]{:S(2)}) async-start(), calls=%async_computation.2 | async-start | bytes 2228224 | tf_op jit(solution)/shard_map/reduce_scatter | solution.py:196
  8.7 6.4 %collective-permute-start = (bf16[2,3,256]{2,0,1:T(2,128)(2,1)S(1)}, bf16[2,3,256]{2,0,1:T(2,128)(2,1)S(1)}, u32[]{:S(2)}, u32[]{:S(2)}) collective-permute-start(bf16[2,3,256]{2,0,1:T(2,128)(2,1)S(1)} %slice.158), channel_id=1, source_target_pairs={{0,1},{1,2},{2,3},{3,4},{4,5},{5,6},{6,7},{7,8},{8,9},{9,10},{10,1... | collective-permute-start | bytes 9224 | tf_op jit(solution)/shard_map/ppermute | solution.py:24
  16.0 129.6 %collective-permute-start.1 = (bf16[2,2,128,1,256]{4,2,1,3,0:T(8,128)(2,1)}, bf16[2,2,128,1,256]{4,2,1,3,0:T(8,128)(2,1)}, u32[]{:S(2)}, u32[]{:S(2)}) collective-permute-start(bf16[2,2,128,1,256]{4,2,1,3,0:T(8,128)(2,1)} %fusion.53), channel_id=1, source_target_pairs={{0,16},{16,0},{1,17},{17,1},{2,18},{18,2},{3,19},{19,3},{4,20},{20... | collective-permute-start | bytes 786440 | tf_op jit(solution)/shard_map/ppermute | solution.py:18
  110.9 0.7 copy-start.3
  111.6 35.0 %collective-permute-start.11 = (bf16[2,2,128,1,256]{4,2,1,3,0:T(8,128)(2,1)S(1)}, bf16[2,2,128,1,256]{4,2,1,3,0:T(8,128)(2,1)S(1)}, u32[]{:S(2)}, u32[]{:S(2)}) collective-permute-start(bf16[2,2,128,1,256]{4,2,1,3,0:T(8,128)(2,1)S(1)} %fusion.52), channel_id=1, source_target_pairs={{0,16},{16,0},{1,17},{17,1},{2,18},{18,2},{3,19},{19,3},{4,20},{20... | collective-permute-start | bytes 786440 | tf_op jit(solution)/shard_map/ppermute | solution.py:18
  149.4 17.2 %collective-permute-start.2 = (bf16[2,2,128,1,256]{4,2,1,3,0:T(8,128)(2,1)}, bf16[2,2,128,1,256]{4,2,1,3,0:T(8,128)(2,1)S(1)}, u32[]{:S(2)}, u32[]{:S(2)}) collective-permute-start(bf16[2,2,128,1,256]{4,2,1,3,0:T(8,128)(2,1)} %get-tuple-element.293), channel_id=1, source_target_pairs={{0,8},{8,0},{1,9},{9,1},{2,10},{10,2},{3,11},{11,3},{4,12},{12,4},... | collective-permute-start | bytes 786440 | tf_op jit(solution)/shard_map/ppermute | solution.py:18
  155.4 19.7 %collective-permute-start.12 = (bf16[2,2,128,1,256]{4,2,1,3,0:T(8,128)(2,1)S(1)}, bf16[2,2,128,1,256]{4,2,1,3,0:T(8,128)(2,1)S(1)}, u32[]{:S(2)}, u32[]{:S(2)}) collective-permute-start(bf16[2,2,128,1,256]{4,2,1,3,0:T(8,128)(2,1)S(1)} %get-tuple-element.273), channel_id=1, source_target_pairs={{0,8},{8,0},{1,9},{9,1},{2,10},{10,2},{3,11},{11,3},{4,12},{12,4},... | collective-permute-start | bytes 786440 | tf_op jit(solution)/shard_map/ppermute | solution.py:18
  166.8 13.6 %collective-permute-start.3 = (bf16[2,2,128,1,256]{4,2,1,3,0:T(8,128)(2,1)S(1)}, bf16[2,2,128,1,256]{4,2,1,3,0:T(8,128)(2,1)S(1)}, u32[]{:S(2)}, u32[]{:S(2)}) collective-permute-start(bf16[2,2,128,1,256]{4,2,1,3,0:T(8,128)(2,1)S(1)} %get-tuple-element.291), channel_id=1, source_target_pairs={{0,4},{4,0},{1,5},{5,1},{2,6},{6,2},{3,7},{7,3},{8,12},{12,8},{9,1... | collective-permute-start | bytes 786440 | tf_op jit(solution)/shard_map/ppermute | solution.py:18
  175.3 10.8 %collective-permute-start.13 = (bf16[2,2,128,1,256]{4,2,1,3,0:T(8,128)(2,1)S(1)}, bf16[2,2,128,1,256]{4,2,1,3,0:T(8,128)(2,1)S(1)}, u32[]{:S(2)}, u32[]{:S(2)}) collective-permute-start(bf16[2,2,128,1,256]{4,2,1,3,0:T(8,128)(2,1)S(1)} %get-tuple-element.271), channel_id=1, source_target_pairs={{0,4},{4,0},{1,5},{5,1},{2,6},{6,2},{3,7},{7,3},{8,12},{12,8},{9,1... | collective-permute-start | bytes 786440 | tf_op jit(solution)/shard_map/ppermute | solution.py:18
  180.7 10.3 %collective-permute-start.4 = (bf16[2,2,128,1,256]{4,2,1,3,0:T(8,128)(2,1)S(1)}, bf16[2,2,128,1,256]{4,2,1,3,0:T(8,128)(2,1)S(1)}, u32[]{:S(2)}, u32[]{:S(2)}) collective-permute-start(bf16[2,2,128,1,256]{4,2,1,3,0:T(8,128)(2,1)S(1)} %get-tuple-element.289), channel_id=1, source_target_pairs={{0,2},{2,0},{1,3},{3,1},{4,6},{6,4},{5,7},{7,5},{8,10},{10,8},{9,1... | collective-permute-start | bytes 786440 | tf_op jit(solution)/shard_map/ppermute | solution.py:18
  186.3 11.0 %collective-permute-start.14 = (bf16[2,2,128,1,256]{4,2,1,3,0:T(8,128)(2,1)S(1)}, bf16[2,2,128,1,256]{4,2,1,3,0:T(8,128)(2,1)S(1)}, u32[]{:S(2)}, u32[]{:S(2)}) collective-permute-start(bf16[2,2,128,1,256]{4,2,1,3,0:T(8,128)(2,1)S(1)} %get-tuple-element.269), channel_id=1, source_target_pairs={{0,2},{2,0},{1,3},{3,1},{4,6},{6,4},{5,7},{7,5},{8,10},{10,8},{9,1... | collective-permute-start | bytes 786440 | tf_op jit(solution)/shard_map/ppermute | solution.py:18
  191.3 11.2 %collective-permute-start.5 = (bf16[2,2,128,1,256]{4,2,1,3,0:T(8,128)(2,1)S(1)}, bf16[2,2,128,1,256]{4,2,1,3,0:T(8,128)(2,1)S(1)}, u32[]{:S(2)}, u32[]{:S(2)}) collective-permute-start(bf16[2,2,128,1,256]{4,2,1,3,0:T(8,128)(2,1)S(1)} %get-tuple-element.287), channel_id=1, source_target_pairs={{0,1},{1,0},{2,3},{3,2},{4,5},{5,4},{6,7},{7,6},{8,9},{9,8},{10,11... | collective-permute-start | bytes 786440 | tf_op jit(solution)/shard_map/ppermute | solution.py:18
  197.5 10.6 %collective-permute-start.15 = (bf16[2,2,128,1,256]{4,2,1,3,0:T(8,128)(2,1)S(1)}, bf16[2,2,128,1,256]{4,2,1,3,0:T(8,128)(2,1)S(1)}, u32[]{:S(2)}, u32[]{:S(2)}) collective-permute-start(bf16[2,2,128,1,256]{4,2,1,3,0:T(8,128)(2,1)S(1)} %get-tuple-element.267), channel_id=1, source_target_pairs={{0,1},{1,0},{2,3},{3,2},{4,5},{5,4},{6,7},{7,6},{8,9},{9,8},{10,11... | collective-permute-start | bytes 786440 | tf_op jit(solution)/shard_map/ppermute | solution.py:18
  218.2 7.3 %collective-permute-start.6 = (bf16[2,2,128,1,256]{4,2,1,3,0:T(8,128)(2,1)S(1)}, bf16[2,2,128,1,256]{4,2,1,3,0:T(8,128)(2,1)S(1)}, u32[]{:S(2)}, u32[]{:S(2)}) collective-permute-start(bf16[2,2,128,1,256]{4,2,1,3,0:T(8,128)(2,1)S(1)} %pad_maximum_fusion.5), channel_id=1, source_target_pairs={{0,1},{1,0},{2,3},{3,2},{4,5},{5,4},{6,7},{7,6},{8,9},{9,8},{10,11... | collective-permute-start | bytes 786440 | tf_op jit(solution)/shard_map/ppermute | solution.py:18
  225.7 10.3 %collective-permute-start.7 = (bf16[2,2,128,1,256]{4,2,1,3,0:T(8,128)(2,1)S(1)}, bf16[2,2,128,1,256]{4,2,1,3,0:T(8,128)(2,1)S(1)}, u32[]{:S(2)}, u32[]{:S(2)}) collective-permute-start(bf16[2,2,128,1,256]{4,2,1,3,0:T(8,128)(2,1)S(1)} %get-tuple-element.281), channel_id=1, source_target_pairs={{0,2},{2,0},{1,3},{3,1},{4,6},{6,4},{5,7},{7,5},{8,10},{10,8},{9,1... | collective-permute-start | bytes 786440 | tf_op jit(solution)/shard_map/ppermute | solution.py:18
  236.3 7.1 %collective-permute-start.8 = (bf16[2,2,128,1,256]{4,2,1,3,0:T(8,128)(2,1)S(1)}, bf16[2,2,128,1,256]{4,2,1,3,0:T(8,128)(2,1)S(1)}, u32[]{:S(2)}, u32[]{:S(2)}) collective-permute-start(bf16[2,2,128,1,256]{4,2,1,3,0:T(8,128)(2,1)S(1)} %get-tuple-element.279), channel_id=1, source_target_pairs={{0,4},{4,0},{1,5},{5,1},{2,6},{6,2},{3,7},{7,3},{8,12},{12,8},{9,1... | collective-permute-start | bytes 786440 | tf_op jit(solution)/shard_map/ppermute | solution.py:18
  243.7 10.7 %collective-permute-start.9 = (bf16[2,2,128,1,256]{4,2,1,3,0:T(8,128)(2,1)S(1)}, bf16[2,2,128,1,256]{4,2,1,3,0:T(8,128)(2,1)S(1)}, u32[]{:S(2)}, u32[]{:S(2)}) collective-permute-start(bf16[2,2,128,1,256]{4,2,1,3,0:T(8,128)(2,1)S(1)} %get-tuple-element.277), channel_id=1, source_target_pairs={{0,8},{8,0},{1,9},{9,1},{2,10},{10,2},{3,11},{11,3},{4,12},{12,4},... | collective-permute-start | bytes 786440 | tf_op jit(solution)/shard_map/ppermute | solution.py:18
  254.4 12.3 %copy-start.4 = (f32[128,256]{1,0:T(8,128)S(1)}, f32[128,256]{1,0:T(8,128)}, u32[]{:S(2)}) copy-start(f32[128,256]{1,0:T(8,128)} %copy-done.3) | copy-start | bytes 393220
  254.6 12.2 %copy-start.2 = (bf16[256,8192]{1,0:T(8,128)(2,1)S(1)}, bf16[256,8192]{1,0:T(8,128)(2,1)}, u32[]{:S(2)}) copy-start(bf16[256,8192]{1,0:T(8,128)(2,1)} %all-gather.2.cloned.1.call-done) | copy-start | bytes 12582916
  254.7 11.8 %collective-permute-start.10 = (bf16[2,2,128,1,256]{4,2,1,3,0:T(8,128)(2,1)S(1)}, bf16[2,2,128,1,256]{4,2,1,3,0:T(8,128)(2,1)S(1)}, u32[]{:S(2)}, u32[]{:S(2)}) collective-permute-start(bf16[2,2,128,1,256]{4,2,1,3,0:T(8,128)(2,1)S(1)} %get-tuple-element.275), channel_id=1, source_target_pairs={{0,16},{16,0},{1,17},{17,1},{2,18},{18,2},{3,19},{19,3},{4,20},{20... | collective-permute-start | bytes 786440 | tf_op jit(solution)/shard_map/ppermute | solution.py:18
  259.6 9.3 %collective-permute-start.16 = (bf16[2,2,128,1,256]{4,2,1,3,0:T(8,128)(2,1)S(1)}, bf16[2,2,128,1,256]{4,2,1,3,0:T(8,128)(2,1)S(1)}, u32[]{:S(2)}, u32[]{:S(2)}) collective-permute-start(bf16[2,2,128,1,256]{4,2,1,3,0:T(8,128)(2,1)S(1)} %pad_maximum_fusion.6), channel_id=1, source_target_pairs={{0,1},{1,0},{2,3},{3,2},{4,5},{5,4},{6,7},{7,6},{8,9},{9,8},{10,11... | collective-permute-start | bytes 786440 | tf_op jit(solution)/shard_map/ppermute | solution.py:18
  269.2 10.3 %collective-permute-start.17 = (bf16[2,2,128,1,256]{4,2,1,3,0:T(8,128)(2,1)S(1)}, bf16[2,2,128,1,256]{4,2,1,3,0:T(8,128)(2,1)S(1)}, u32[]{:S(2)}, u32[]{:S(2)}) collective-permute-start(bf16[2,2,128,1,256]{4,2,1,3,0:T(8,128)(2,1)S(1)} %get-tuple-element.261), channel_id=1, source_target_pairs={{0,2},{2,0},{1,3},{3,1},{4,6},{6,4},{5,7},{7,5},{8,10},{10,8},{9,1... | collective-permute-start | bytes 786440 | tf_op jit(solution)/shard_map/ppermute | solution.py:18
  279.8 7.1 %collective-permute-start.18 = (bf16[2,2,128,1,256]{4,2,1,3,0:T(8,128)(2,1)S(1)}, bf16[2,2,128,1,256]{4,2,1,3,0:T(8,128)(2,1)S(1)}, u32[]{:S(2)}, u32[]{:S(2)}) collective-permute-start(bf16[2,2,128,1,256]{4,2,1,3,0:T(8,128)(2,1)S(1)} %get-tuple-element.259), channel_id=1, source_target_pairs={{0,4},{4,0},{1,5},{5,1},{2,6},{6,2},{3,7},{7,3},{8,12},{12,8},{9,1... | collective-permute-start | bytes 786440 | tf_op jit(solution)/shard_map/ppermute | solution.py:18
  287.2 11.4 %collective-permute-start.19 = (bf16[2,2,128,1,256]{4,2,1,3,0:T(8,128)(2,1)S(1)}, bf16[2,2,128,1,256]{4,2,1,3,0:T(8,128)(2,1)S(1)}, u32[]{:S(2)}, u32[]{:S(2)}) collective-permute-start(bf16[2,2,128,1,256]{4,2,1,3,0:T(8,128)(2,1)S(1)} %get-tuple-element.257), channel_id=1, source_target_pairs={{0,8},{8,0},{1,9},{9,1},{2,10},{10,2},{3,11},{11,3},{4,12},{12,4},... | collective-permute-start | bytes 786440 | tf_op jit(solution)/shard_map/ppermute | solution.py:18
  298.8 47.7 %copy-start.1 = (bf16[128,8192]{1,0:T(8,128)(2,1)S(1)}, bf16[128,8192]{1,0:T(8,128)(2,1)}, u32[]{:S(2)}) copy-start(bf16[128,8192]{1,0:T(8,128)(2,1)} %param.13) | copy-start | bytes 6291460
  298.8 13.6 %collective-permute-start.20 = (bf16[2,2,128,1,256]{4,2,1,3,0:T(8,128)(2,1)S(1)}, bf16[2,2,128,1,256]{4,2,1,3,0:T(8,128)(2,1)S(1)}, u32[]{:S(2)}, u32[]{:S(2)}) collective-permute-start(bf16[2,2,128,1,256]{4,2,1,3,0:T(8,128)(2,1)S(1)} %get-tuple-element.255), channel_id=1, source_target_pairs={{0,16},{16,0},{1,17},{17,1},{2,18},{18,2},{3,19},{19,3},{4,20},{20... | collective-permute-start | bytes 786440 | tf_op jit(solution)/shard_map/ppermute | solution.py:18
  312.8 4.7 %collective-permute-start.21 = (f32[2,3,256]{2,0,1:T(2,128)S(1)}, f32[2,3,256]{2,0,1:T(2,128)S(1)}, u32[]{:S(2)}, u32[]{:S(2)}) collective-permute-start(f32[2,3,256]{2,0,1:T(2,128)S(1)} %slice.482), channel_id=1, source_target_pairs={{1,0},{2,1},{3,2},{4,3},{5,4},{6,5},{7,6},{8,7},{9,8},{10,9},{11,1... | collective-permute-start | bytes 18440 | tf_op jit(solution)/shard_map/ppermute | solution.py:24
Sparse Core Ops, SparseCore 0:
  11.0 96.1 all-gather.1
  269.0 77.4 reduce-scatter.1
where the time goes:
time: 357 us; the launch traced here: 353 us
  waiting for transfers between devices  193 us (54%)
  starting transfers between devices  82.5 us (23%)
  other arithmetic  41.7 us (12%)
  matrix products  17 us (5%)
  between operations  15.9 us (4%)
    ppermute x20, waiting for transfers between devices, swapped(): return lax.ppermute(block, axis, route)  82.5 us
    all_gather x1, waiting for transfers between devices, per_device(): w_full = lax.all_gather(w_out, 'ctx', axis=1, tiled=True)  78.4 us
    ppermute x20, starting transfers between devices, swapped(): return lax.ppermute(block, axis, route)  77.2 us
    reduce_scatter x1, waiting for transfers between devices, per_device(): lax.psum_scatter(partial_sum.astype(jnp.bfloat16), 'fsdp', scatter_dimens...  28.2 us
    mul x16, other arithmetic, add_mode(): denom_im = decay_now * full_sine  12.1 us
    mul x16, other arithmetic, add_mode(): lax.dynamic_slice_in_dim(residues, mode_index, 1, 1)[:, 0]  11.8 us
  transfers between devices with their start and end apart: 24, of which 19 were waited for; matrix products, arithmetic and copies ran while one was open for 13% of the time, Pallas kernels for 0%

commit v1 on v0

v1 whole, which is shorter than its diff:
```python
import jax
import jax.numpy as jnp
from jax import lax
from jax.experimental import pallas as pl
from jax.experimental.pallas import tpu as pltpu
from jax.sharding import PartitionSpec as P

T = 128


def rows_iota(n):
    return lax.broadcasted_iota(jnp.int32, (n, 1), 0).astype(jnp.float32)


def forward_kernel(x_ref, a_ref, w_ref, y_ref, s_ref, h_ref, pad_ref):
    x = x_ref[...]
    k = rows_iota(T)

    def mode(n, h):
        a = a_ref[pl.ds(n, 1), :]
        back = jnp.exp(-a * (T - 1 - k))
        s_ref[pl.ds(n, 1), :] = jnp.sum(back * x, axis=0, keepdims=True)
        return h + w_ref[pl.ds(n, 1), :] * jnp.exp(-a * k)

    h_ref[...] = lax.fori_loop(0, 16, mode, jnp.zeros_like(x))
    row = lax.broadcasted_iota(jnp.int32, (T, 1), 0)
    for r in range(8):
        pad_ref[r, :T, :] = jnp.zeros_like(x)
        pad_ref[r, T:, :] = jnp.where(row >= r, pltpu.roll(x, r, 0), 0.0) if r else x

    def taps(q, y):
        for r in range(8):
            start = pl.multiple_of(T - 8 * q, 8)
            y = y + h_ref[pl.ds(8 * q + r, 1), :] * pad_ref[r, pl.ds(start, T), :]
        return y

    y_ref[...] = lax.fori_loop(0, 16, taps, jnp.zeros_like(x))


def backward_kernel(x_ref, a_ref, h_ref, y_ref, s_ref, pad_ref):
    x = x_ref[...]
    k = rows_iota(T)

    def mode(n, c):
        a = a_ref[pl.ds(n, 1), :]
        s_ref[pl.ds(n, 1), :] = jnp.sum(jnp.exp(-a * k) * x, axis=0, keepdims=True)
        return c

    lax.fori_loop(0, 16, mode, 0)
    row = lax.broadcasted_iota(jnp.int32, (T, 1), 0)
    for r in range(8):
        pad_ref[r, T:, :] = jnp.zeros_like(x)
        pad_ref[r, :T, :] = jnp.where(row < T - r, pltpu.roll(x, T - r, 0), 0.0) if r else x

    def taps(q, y):
        for r in range(8):
            start = pl.multiple_of(8 * q, 8)
            y = y + h_ref[pl.ds(8 * q + r, 1), :] * pad_ref[r, pl.ds(start, T), :]
        return y

    y_ref[...] = lax.fori_loop(0, 16, taps, jnp.zeros_like(x))


def shifted(block, axis, distance):
    devices = range(lax.axis_size(axis))
    route = [(i - distance, i) for i in devices if i - distance in devices]
    return lax.ppermute(block, axis, route)


def per_device(featurized, short_taps, residues, decay_rates, w_out, grad_out):
    f32 = jnp.float32
    shape = jax.ShapeDtypeStruct((T, 256), f32)
    modes = jax.ShapeDtypeStruct((16, 256), f32)
    w_full = lax.all_gather(w_out, "ctx", axis=1, tiled=True)
    a = decay_rates.T
    weight = residues.T * jnp.sqrt(a)
    me = lax.axis_index("ctx")
    others = jnp.arange(32)[:, None, None]
    before = shifted(featurized[T - 2 :], "ctx", 1)
    extended = jnp.concatenate([before, featurized], axis=0).astype(f32)
    mixed = (
        short_taps[0] * extended[2:]
        + short_taps[1] * extended[1 : T + 1]
        + short_taps[2] * extended[:T]
    )
    query, key, value = mixed[:, 0], mixed[:, 1], mixed[:, 2]
    carried = key * value
    local, states, h = pl.pallas_call(
        forward_kernel,
        out_shape=(shape, modes, shape),
        scratch_shapes=[pltpu.VMEM((8, 2 * T, 256), f32)],
    )(carried, a, weight)
    all_states = lax.all_gather(states, "ctx")
    gap = me - 1 - others
    entering = jnp.sum(
        jnp.where(gap >= 0, jnp.exp(-a * (T * jnp.maximum(gap, 0)).astype(f32)), 0.0) * all_states, axis=0
    )
    k = rows_iota(T)
    spread = weight * entering
    convolved = local
    for n in range(16):
        convolved = convolved + spread[n] * jnp.exp(-a[n] * (k + 1))
    gated = (query * convolved).astype(jnp.bfloat16)
    partial = jnp.dot(gated, w_full, preferred_element_type=f32)
    block_output = lax.psum_scatter(
        partial.astype(jnp.bfloat16), "fsdp", scatter_dimension=1, tiled=True
    )
    grad_gated = lax.dot_general(
        grad_out, w_full, (((1,), (1,)), ((), ())), preferred_element_type=f32
    )
    grad_query = grad_gated * convolved
    grad_conv = grad_gated * query
    local_b, states_b = pl.pallas_call(
        backward_kernel,
        out_shape=(shape, modes),
        scratch_shapes=[pltpu.VMEM((8, 2 * T, 256), f32)],
    )(grad_conv, a, h)
    all_b = lax.all_gather(states_b, "ctx")
    gap = others - me - 1
    leaving = jnp.sum(
        jnp.where(gap >= 0, jnp.exp(-a * (T * jnp.maximum(gap, 0)).astype(f32)), 0.0) * all_b, axis=0
    )
    spread = weight * leaving
    grad_carried = local_b
    for n in range(16):
        grad_carried = grad_carried + spread[n] * jnp.exp(-a[n] * (T - k))
    grad_mixed = jnp.stack([grad_query, grad_carried * value, grad_carried * key], axis=1)
    following = shifted(grad_mixed[:2], "ctx", -1)
    padded = jnp.concatenate([grad_mixed, following], axis=0)
    grad_features = (
        short_taps[0] * padded[:T] + short_taps[1] * padded[1 : T + 1] + short_taps[2] * padded[2:]
    ).astype(jnp.bfloat16)
    return (block_output, grad_features)


def solution(mesh):
    placed = (
        P("ctx", None, "fsdp"),
        P(None, None, "fsdp"),
        P("fsdp", None),
        P("fsdp", None),
        P("fsdp", "ctx"),
        P("ctx", None),
    )
    return jax.shard_map(
        per_device,
        mesh=mesh,
        in_specs=placed,
        out_specs=(P("ctx", "fsdp"), P("ctx", None, "fsdp")),
        check_vma=False,
    )
```

time: 357 us -> 288 us (0.81)
  starting transfers between devices: 82.5 us -> 5.29 us
  blocking collectives: 0 us -> 72.8 us
  other arithmetic: 41.7 us -> 5.56 us
  waiting for transfers between devices: 193 us -> 169 us
  Pallas kernels: 0 us -> 8.53 us
  matrix products: 17 us -> 9.22 us
    ppermute x20 -> x0, waiting for transfers between devices: 82.5 us -> none  [swapped(): return lax.ppermute(block, axis, route)]
    ppermute x20 -> x0, starting transfers between devices: 77.2 us -> none  [swapped(): return lax.ppermute(block, axis, route)]
    all_gather x0 -> x2, blocking collectives: none -> 72.8 us  [the longest x1 37.3 us: per_device(): all_b = lax.all_gather(states_b, 'ctx')]
    reduce_scatter x1, waiting for transfers between devices: 28.2 us -> 79.8 us  [per_device(): lax.psum_scatter(partial.astype(jnp.bfloat16), 'fsdp', scatter_dimension=...]
    mul x84 -> x1, other arithmetic: 26 us -> 0.01 us  [per_device(): spread = weight * leaving]
    pallas_call x0 -> x2, Pallas kernels: none -> 8.53 us  [the longest x1 4.44 us: per_device(): pl.pallas_call(forward_kernel, out_shape=(shape, modes, shape), scratch_s...]
    dot_general x17 -> x1, matrix products: 13.3 us -> 4.84 us  [per_device(): partial = jnp.dot(gated, w_full, preferred_element_type=f32)]
    all_gather x1, waiting for transfers between devices: 78.4 us -> 85.6 us  [per_device(): w_full = lax.all_gather(w_out, 'ctx', axis=1, tiled=True)]
  transfers between devices with their start and end apart: 24 -> 4, of which waited for: 19 -> 3; matrix products, arithmetic and copies ran while one was open for 13% -> 2% of each run, Pallas kernels for 0% -> 0%
where the time goes in v1:
time: 288 us; the launch traced here: 286 us
  waiting for transfers between devices  169 us (59%)
  blocking collectives  72.8 us (25%)
  between operations  14.2 us (5%)
  matrix products  9.22 us (3%)
  Pallas kernels  8.53 us (3%)
  other arithmetic  5.56 us (2%)
  starting transfers between devices  5.29 us (2%)
    all_gather x1, waiting for transfers between devices, per_device(): w_full = lax.all_gather(w_out, 'ctx', axis=1, tiled=True)  85.6 us
    reduce_scatter x1, waiting for transfers between devices, per_device(): lax.psum_scatter(partial.astype(jnp.bfloat16), 'fsdp', scatter_dimension=...  79.8 us
    all_gather x1, blocking collectives, per_device(): all_b = lax.all_gather(states_b, 'ctx')  37.3 us
    all_gather x1, blocking collectives, per_device(): all_states = lax.all_gather(states, 'ctx')  35.5 us
  transfers between devices with their start and end apart: 4, of which 3 were waited for; matrix products, arithmetic and copies ran while one was open for 2% of the time, Pallas kernels for 0%

profile of v1, /device:TPU:1, one launch (start us, length us, event | category | flops | bytes accessed | tf_op | source)
XLA Modules:
  0.0 286.3 jit_solution(14080468177074942337)
XLA Ops:
  7.2 0.0 copy-start
  7.2 0.0 all-gather.4.cloned.1.call-start
  7.2 0.7 all-gather.4.cloned.1.call-update
  7.9 0.0 reduce-scatter.2.cloned.1.call-start
  8.0 0.7 slice.203
  8.7 3.9 %collective-permute-start = (bf16[2,3,256]{2,0,1:T(2,128)(2,1)S(1)}, bf16[2,3,256]{2,0,1:T(2,128)(2,1)S(1)}, u32[]{:S(2)}, u32[]{:S(2)}) collective-permute-start(bf16[2,3,256]{2,0,1:T(2,128)(2,1)S(1)} %slice.203), channel_id=1, source_target_pairs={{0,1},{1,2},{2,3},{3,4},{4,5},{5,6},{6,7},{7,8},{8,9},{9,10},{10,1... | collective-permute-start | bytes 9224 | tf_op jit(solution)/shard_map/ppermute | solution.py:67
  12.7 0.7 slice_bitcast_fusion.5
  13.4 1.0 slice_negate_fusion.15
  14.4 1.3 bitcast_negate_fusion
  15.8 0.0 collective-permute-done
  15.8 1.0 maximum_convert_fusion
  16.7 0.1 fusion.3
  16.9 0.0 copy-start.1
  16.9 85.6 %all-gather.4.cloned.1.call-done = bf16[256,8192]{1,0:T(8,128)(2,1)} async-done(((bf16[256,256]{1,0:T(8,128)(2,1)}), bf16[256,8192]{1,0:T(8,128)(2,1)}) %all-gather.4.cloned.1.call-update) | async-done | bytes 4194320 | tf_op jit(solution)/shard_map/all_gather | solution.py:74
  102.4 0.0 copy-done
  102.4 4.4 %fusion.5 = (f32[128,256]{1,0:T(8,128)}, f32[128,256]{1,0:T(8,128)}, f32[128,256]{1,0:T(8,128)S(1)}) fusion(f32[128,3,256]{2,0,1:T(8,128)S(1)} %fusion.3, bf16[128,8192]{1,0:T(8,128)(2,1)S(1)} %copy-done, bf16[256,8192]{1,0:T(8,128)(2,1)} %all-gather.4.cloned.1.call-done), kind=kOutput, calls=%fused_computation.25 | convolution fusion | flops 536936448 | bytes 7077888 | tf_op jit(solution)/shard_map/dot_general | solution.py:108
  106.8 4.4 %shard_map.77 = (f32[128,256]{1,0:T(8,128)}, f32[16,256]{1,0:T(8,128)}, f32[128,256]{1,0:T(8,128)}) custom-call(f32[128,256]{1,0:T(8,128)} %get-tuple-element.17.x_ref, f32[16,256]{1,0:T(8,128)} %bitcast.92, f32[16,256]{1,0:T(8,128)} %get-tuple-element.69.w_ref), custom_call_target="tpu_custom_call" | custom-call | tf_op jit(solution)/shard_map/pallas_call | solution.py:88
  111.2 4.1 %shard_map.78 = (f32[128,256]{1,0:T(8,128)}, f32[16,256]{1,0:T(8,128)}) custom-call(f32[128,256]{1,0:T(8,128)} %get-tuple-element.16.x_ref, f32[16,256]{1,0:T(8,128)} %bitcast.93, f32[128,256]{1,0:T(8,128)} %get-tuple-element.9.h_ref), custom_call_target="tpu_custom_call" | custom-call | tf_op jit(solution)/shard_map/pallas_call | solution.py:113
  115.3 37.3 %all-gather.1 = f32[512,256]{1,0:T(8,128)S(1)} all-gather(f32[16,256]{1,0:T(8,128)} %get-tuple-element.11), channel_id=3, replica_groups=mesh['fsdp'=16,'ctx'=32] {'ctx'}, dimensions={0}, use_global_device_ids=true | all-gather | bytes 540672 | tf_op jit(solution)/shard_map/all_gather | solution.py:118
  152.6 35.5 %all-gather = f32[512,256]{1,0:T(8,128)S(1)} all-gather(f32[16,256]{1,0:T(8,128)} %get-tuple-element.8), channel_id=2, replica_groups=mesh['fsdp'=16,'ctx'=32] {'ctx'}, dimensions={0}, use_global_device_ids=true | all-gather | bytes 540672 | tf_op jit(solution)/shard_map/all_gather | solution.py:93
  188.1 0.3 multiply_reduce_fusion
  188.4 0.0 copy-done.1
  188.5 0.0 copy-start.3
  188.5 0.0 copy-start.2
  188.5 4.8 %convolution_convert_fusion = bf16[128,8192]{1,0:T(8,128)(2,1)} fusion(bf16[256,8192]{1,0:T(8,128)(2,1)} %all-gather.4.cloned.1.call-done, f32[128,3,256]{2,0,1:T(8,128)S(1)} %fusion.3, f32[128,256]{1,0:T(8,128)} %get-tuple-element.7, f32[256]{0:T(256)S(1)} %bitcast.139, f32[256]{0:T(256)S(1)} %bitcast.144, f32[256]{0:T(256)S(1)} %bitcast.97, ...), kind=kOutput, calls=%fused_computation | convolution fusion | flops 539557888 | bytes 6586880 | tf_op jit(solution)/shard_map/dot_general | solution.py:104
  193.3 0.0 reduce-scatter.2.cloned.1.call-update
  193.4 0.0 copy-done.3
  193.4 0.4 multiply_bitcast_fusion.1
  193.9 0.0 copy-done.2
  193.9 0.4 multiply_bitcast_fusion.2
  194.4 1.3 collective-permute-start.1
  195.7 3.1 %collective-permute-done.1 = f32[2,3,256]{2,0,1:T(2,128)S(1)} collective-permute-done((f32[2,3,256]{2,0,1:T(2,128)S(1)}, f32[2,3,256]{2,0,1:T(2,128)S(1)}, u32[]{:S(2)}, u32[]{:S(2)}) %collective-permute-start.1) | collective-permute-done | bytes 6176 | tf_op jit(solution)/shard_map/ppermute | solution.py:67
  198.8 0.8 fusion.1
  199.6 79.8 %reduce-scatter.2.cloned.1.call-done = bf16[128,512]{1,0:T(8,128)(2,1)} async-done(((bf16[128,8192]{1,0:T(8,128)(2,1)}), bf16[128,512]{1,0:T(8,128)(2,1)}) %reduce-scatter.2.cloned.1.call-update) | async-done | bytes 131088 | tf_op jit(solution)/shard_map/reduce_scatter | solution.py:105
  (11 shorter events, 0.1 us)
Async XLA Ops:
  7.2 95.3 %copy-start = (bf16[128,8192]{1,0:T(8,128)(2,1)S(1)}, bf16[128,8192]{1,0:T(8,128)(2,1)}, u32[]{:S(2)}) copy-start(bf16[128,8192]{1,0:T(8,128)(2,1)} %param.11) | copy-start | bytes 6291460
  7.2 95.2 %all-gather.4.cloned.1.call-start = ((), (), s32[]{:S(2)}) async-start(), calls=%async_computation.1 | async-start | bytes 4325376 | tf_op jit(solution)/shard_map/all_gather | solution.py:74
  7.9 271.5 %reduce-scatter.2.cloned.1.call-start = ((), (), s32[]{:S(2)}) async-start(), calls=%async_computation.2 | async-start | bytes 2228224 | tf_op jit(solution)/shard_map/reduce_scatter | solution.py:105
  8.7 7.1 %collective-permute-start = (bf16[2,3,256]{2,0,1:T(2,128)(2,1)S(1)}, bf16[2,3,256]{2,0,1:T(2,128)(2,1)S(1)}, u32[]{:S(2)}, u32[]{:S(2)}) collective-permute-start(bf16[2,3,256]{2,0,1:T(2,128)(2,1)S(1)} %slice.203), channel_id=1, source_target_pairs={{0,1},{1,2},{2,3},{3,4},{4,5},{5,6},{6,7},{7,8},{8,9},{9,10},{10,1... | collective-permute-start | bytes 9224 | tf_op jit(solution)/shard_map/ppermute | solution.py:67
  16.9 171.5 %copy-start.1 = (f32[16,256]{1,0:T(8,128)S(1)}, f32[16,256]{1,0:T(8,128)}, u32[]{:S(2)}) copy-start(f32[16,256]{1,0:T(8,128)} %get-tuple-element.69.w_ref) | copy-start | bytes 49156
  188.5 4.9 %copy-start.3 = (f32[128,256]{1,0:T(8,128)S(1)}, f32[128,256]{1,0:T(8,128)}, u32[]{:S(2)}) copy-start(f32[128,256]{1,0:T(8,128)} %get-tuple-element.10) | copy-start | bytes 393220
  188.5 5.4 %copy-start.2 = (f32[128,256]{1,0:T(8,128)S(1)}, f32[128,256]{1,0:T(8,128)}, u32[]{:S(2)}) copy-start(f32[128,256]{1,0:T(8,128)} %get-tuple-element.7) | copy-start | bytes 393220
  194.4 4.4 %collective-permute-start.1 = (f32[2,3,256]{2,0,1:T(2,128)S(1)}, f32[2,3,256]{2,0,1:T(2,128)S(1)}, u32[]{:S(2)}, u32[]{:S(2)}) collective-permute-start(f32[2,3,256]{2,0,1:T(2,128)S(1)} %slice.317), channel_id=1, source_target_pairs={{1,0},{2,1},{3,2},{4,3},{5,4},{6,5},{7,6},{8,7},{9,8},{10,9},{11,1... | collective-permute-start | bytes 18440 | tf_op jit(solution)/shard_map/ppermute | solution.py:67
Sparse Core Ops, SparseCore 0:
  11.0 91.3 all-gather.3
  193.5 85.9 reduce-scatter.1

commit v2 on v1

v2 whole, which is shorter than its diff:
```python
import heapq

import jax
import jax.numpy as jnp
from jax import lax
from jax.experimental import pallas as pl
from jax.experimental.pallas import tpu as pltpu
from jax.sharding import PartitionSpec as P

T = 128
C = 256
MODES = 16
NZ, NX, NY = 8, 4, 8
F32 = jnp.float32
BF16 = jnp.bfloat16
MESH = pl.DeviceIdType.MESH

Z_FIRST = 160
PART = {"z": (0, Z_FIRST), "x": (Z_FIRST, C - Z_FIRST)}
STEP = ((1, 0), (-1, 0), (0, 1), (0, -1))


def next_messages(part, dz, dx, rows, arrived):
    first, second = ((0, 1), (2, 3)) if part == "z" else ((2, 3), (0, 1))
    if arrived is None:
        ways = first + second
    elif arrived in first:
        ways = (arrived,) + second
    else:
        ways = (arrived,)
    start, count = PART[part]
    low = count // 32 * 16
    half = {0: (start, low), 1: (start + low, count - low)}
    sends = []
    for way in ways:
        farthest, now = (NZ // 2, dz) if way < 2 else (NX // 2, dx)
        distance = abs(now) + 1
        if distance > farthest:
            continue
        use, place = rows, (-distance if way % 2 == 0 else distance)
        if distance == farthest:
            place = distance
            if rows == PART[part]:
                use = half[way % 2]
            elif rows != half[way % 2]:
                continue
        sends.append((part, place if way < 2 else dz, place if way >= 2 else dx, way) + use)
    return sends


def gather_schedule():
    free, queue, order = [0.0] * 4, [], []

    def issue(now, messages):
        for m in messages:
            begin = max(free[m[3]], now)
            free[m[3]] = begin + m[5] * 2 * C / 46.5e3
            heapq.heappush(queue, (free[m[3]] + 1.7, m))

    own_z = next_messages("z", 0, 0, PART["z"], None)
    own_x = next_messages("x", 0, 0, PART["x"], None)
    opening = own_z[:2] + own_x[:2] + own_z[2:] + own_x[2:]
    issue(0.0, opening)
    while queue:
        now, m = heapq.heappop(queue)
        after = next_messages(m[0], m[1], m[2], m[4:], m[3])
        order.append((now, m, after))
        issue(now, after)
    return opening, order


OPENING, ORDER = gather_schedule()
SLOT = {m: i for i, (_, m, _) in enumerate(ORDER)}
ROW_READY = {d % NZ: max(t for t, m, _ in ORDER if m[1] % NZ == d % NZ) for d in range(NZ)}
ROW_ORDER = sorted(ROW_READY, key=ROW_READY.get)


def kernel(
    feats_ref, taps_ref, a_ref, res_ref, w_ref, go_ref, out_ref, gf_ref,
    w_all, go_all, near, far, h_ref, pad_ref, mix_ref, conv_ref, gg_ref, acc_ref,
    tail_ref, halo_ref, state_ref, x_states, z_states, mine_ref, pair_ref, send_ref, land_ref, weight_ref,
    own_sem, w_send, w_recv, halo_send, halo_recv, x_send, x_recv, z_send, z_recv,
    pair_send, pair_recv, y_send, y_recv,
):
    f, k = lax.axis_index("fsdp"), lax.axis_index("ctx")
    y, core = f // 2, f % 2
    z, x = k // NX, k % NX

    def at(dz, dx):
        return lax.rem(z + dz + NZ, NZ) * NX + lax.rem(x + dx + NX, NX)

    def ctx(index):
        return {"fsdp": f, "ctx": index}

    def remote(src, dst, send, recv, device):
        return pltpu.make_async_remote_copy(
            src_ref=src, dst_ref=dst, send_sem=send, recv_sem=recv, device_id=device, device_id_type=MESH
        )

    following, previous = lax.rem(k + 1, NZ * NX), lax.rem(k + NZ * NX - 1, NZ * NX)
    partner = {"fsdp": y * 2 + 1 - core, "ctx": k}

    barrier = pltpu.get_barrier_semaphore()
    greeted = [ctx(at(*s)) for s in STEP] + [ctx(following), ctx(previous), partner]
    greeted += [{"fsdp": lax.rem(y + d, NY) * 2 + core, "ctx": k} for d in range(1, NY)]
    greeted += [ctx(at(0, 2))] + [ctx(at(d, 0)) for d in range(2, NZ - 1)]
    for device in greeted:
        pl.semaphore_signal(barrier, inc=1, device_id=device, device_id_type=MESH)
    pl.semaphore_wait(barrier, len(greeted))

    pending = []

    def start_message(m, own):
        part, dz, dx, way, row, rows = m
        sz, sx = STEP[way]
        block = at(sz + dz, sx + dx)
        src = w_ref.at[pl.ds(row, rows), :] if own else w_all.at[block, pl.ds(row, rows), :]
        copy = remote(
            src, w_all.at[block, pl.ds(row, rows), :], w_send.at[SLOT[m]], w_recv.at[SLOT[m]], ctx(at(sz, sx))
        )
        copy.start()
        pending.append(copy)

    for m in OPENING:
        start_message(m, True)
    own_w = pltpu.make_async_copy(w_ref, w_all.at[k], own_sem.at[0])
    own_w.start()
    own_go = pltpu.make_async_copy(go_ref, go_all, own_sem.at[1])
    own_go.start()

    def relay(m, after):
        _, dz, dx, _, row, rows = m
        block = w_all.at[at(dz, dx), pl.ds(row, rows), :]
        remote(block, block, w_send.at[SLOT[m]], w_recv.at[SLOT[m]], ctx(k)).wait_recv()
        for later in after:
            start_message(later, False)

    rows = lax.broadcasted_iota(jnp.int32, (T, 1), 0)
    steps = rows.astype(F32)

    def halo_copy(which, device):
        return remote(
            tail_ref.at[which], halo_ref.at[which], halo_send.at[which], halo_recv.at[which], ctx(device)
        )

    def send_tail():
        for j in range(3):
            last = feats_ref[j, T - 16 :, :].astype(F32)
            tail_ref[0, 2 * j : 2 * j + 2, :] = last[14:16]
        copy = halo_copy(0, following)
        copy.start()
        pending.append(copy)

    def tables(low):
        def body(n, c):
            a = a_ref[pl.ds(n, 1), :]
            scale = res_ref[pl.ds(n, 1), :] * jnp.sqrt(a)
            weight_ref[pl.ds(n, 1), :] = scale
            e = jnp.exp(-a * steps)
            near[n] = e
            far[n] = jnp.exp(-a * (T - 1 - steps))
            h_ref[...] += scale * e
            return c

        lax.fori_loop(low, low + 4, body, 0)

    def clear():
        h_ref[...] = jnp.zeros_like(h_ref)
        gg_ref[...] = jnp.zeros_like(gg_ref)

    def end_state(table, signal_ref, which):
        def body(n, c):
            state_ref[which, pl.ds(n, 1), :] = jnp.sum(table[n] * signal_ref[...], axis=0, keepdims=True)
            return c

        lax.fori_loop(0, MODES, body, 0)

    def send_x(which):
        for d in range(1, NX):
            copy = remote(
                state_ref.at[which], x_states.at[which, x], x_send.at[which, d], x_recv.at[which, x], ctx(at(0, d))
            )
            copy.start()
            pending.append(copy)

    def mix():
        halo_copy(0, following).wait_recv()
        for j in range(3):
            now = feats_ref[j].astype(F32)
            one = jnp.where(k > 0, halo_ref[0, 2 * j + 1 : 2 * j + 2, :], 0.0)
            two = jnp.where(k > 0, halo_ref[0, 2 * j : 2 * j + 1, :], 0.0)
            back1 = jnp.where(rows == 0, one, pltpu.roll(now, 1, 0))
            back2 = jnp.where(rows == 0, two, jnp.where(rows == 1, one, pltpu.roll(now, 2, 0)))
            mix_ref[j] = (
                taps_ref[0, j : j + 1, :] * now + taps_ref[1, j : j + 1, :] * back1 + taps_ref[2, j : j + 1, :] * back2
            )
        acc_ref[...] = mix_ref[1] * mix_ref[2]

    def forward_send():
        end_state(far, acc_ref, 0)
        send_x(0)

    def shift_copies(which, low):
        value = acc_ref[...]
        for r in range(low, low + 4):
            if which == 0:
                pad_ref[r, :T, :] = jnp.zeros_like(value)
                pad_ref[r, T:, :] = jnp.where(rows >= r, pltpu.roll(value, r, 0), 0.0) if r else value
            else:
                pad_ref[r, T:, :] = jnp.zeros_like(value)
                pad_ref[r, :T, :] = jnp.where(rows < T - r, pltpu.roll(value, T - r, 0), 0.0) if r else value

    def local_taps(which, low, high, dst, begin):
        def body(q, total):
            for r in range(8):
                start = pl.multiple_of((T - 8 * q) if which == 0 else 8 * q, 8)
                total = total + h_ref[pl.ds(8 * q + r, 1), :] * pad_ref[r, pl.ds(start, T), :]
            return total

        first = jnp.zeros((T, C), F32) if begin else dst[...]
        dst[...] = lax.fori_loop(low, high, body, first)

    def combine_x(which):
        x_states[which, x] = state_ref[which]
        for d in range(1, NX):
            other = lax.rem(x + d, NX)
            remote(
                state_ref.at[which], x_states.at[which, other], x_send.at[which, d], x_recv.at[which, other], ctx(k)
            ).wait_recv()
        a = a_ref[...]
        entering, total = jnp.zeros_like(a), jnp.zeros_like(a)
        for j in range(NX):
            gap = (x - 1 - j) if which == 0 else (j - x - 1)
            reach = (NX - 1 - j) if which == 0 else j
            decay = jnp.exp(-a * (T * jnp.maximum(gap, 0)).astype(F32))
            state = x_states[which, j]
            entering = entering + jnp.where(gap >= 0, decay * state, 0.0)
            total = total + jnp.exp(-a * float(T * reach)) * state
        state_ref[2 + which] = entering
        state_ref[4 + which] = total
        for d in range(1, NZ):
            to = lax.rem(z + d, NZ)

            @pl.when((to > z) if which == 0 else (to < z))
            def _(d=d):
                z_copy(which, d).start()

    def z_copy(which, d):
        return remote(
            state_ref.at[4 + which], z_states.at[which, z], z_send.at[which, d], z_recv.at[which, z], ctx(at(d, 0))
        )

    def combine_z(which):
        a = a_ref[...]
        state_ref[6] = jnp.zeros_like(a)
        for d in range(1, NZ):
            other = lax.rem(z + d, NZ)

            @pl.when((other < z) if which == 0 else (other > z))
            def _(d=d, other=other):
                remote(
                    state_ref.at[4 + which],
                    z_states.at[which, other],
                    z_send.at[which, d],
                    z_recv.at[which, other],
                    ctx(at(d, 0)),
                ).wait_recv()
                gap = (z - 1 - other) if which == 0 else (other - z - 1)
                state_ref[6] += jnp.exp(-a * (NX * T * gap).astype(F32)) * z_states[which, other]

        inside = x if which == 0 else NX - 1 - x
        entering = state_ref[2 + which] + jnp.exp(-a * (T * inside).astype(F32)) * state_ref[6]
        state_ref[7] = weight_ref[...] * jnp.exp(-a) * entering

    def boundary(table, dst):
        def body(n, total):
            return total + table[n] * state_ref[7, pl.ds(n, 1), :]

        dst[...] = lax.fori_loop(0, MODES, body, dst[...])

    def gate():
        combine_z(0)
        boundary(near, conv_ref)
        own_w.wait()
        own_go.wait()

    def project(dz):
        row = lax.rem(z + dz, NZ)
        gated = (mix_ref[0] * conv_ref[...]).astype(BF16)

        def body(i, c):
            block = row * NX + i
            w = w_all[block]
            part = jnp.dot(gated, w, preferred_element_type=F32)
            mine_ref[row, i] = part.astype(BF16)
            columns = pl.ds(pl.multiple_of(block * C, C), C)
            gg_ref[...] += lax.dot_general(
                go_all[:, columns], w, (((1,), (1,)), ((), ())), preferred_element_type=F32
            )
            return c

        lax.fori_loop(0, NX, body, 0)
        copy = pair_copy(dz)
        copy.start()
        pending.append(copy)

    def pair_copy(dz):
        row = lax.rem(z + dz, NZ)
        theirs = pl.ds((1 - core) * 2, 2)
        return remote(mine_ref.at[row, theirs], pair_ref.at[row], pair_send.at[row], pair_recv.at[row], partner)

    def y_copy(row):
        return remote(
            send_ref.at[row], land_ref.at[y], y_send.at[row], y_recv.at[y], {"fsdp": row * 2 + core, "ctx": k}
        )

    def pass_on(dz):
        row = lax.rem(z + dz, NZ)
        pair_copy(dz).wait_recv()
        for i in range(2):
            total = mine_ref[row, core * 2 + i].astype(F32) + pair_ref[row, i].astype(F32)
            send_ref[row, i] = total.astype(BF16)

        @pl.when(row != y)
        def _():
            y_copy(row).start()

    def finish_output():
        for i in range(2):
            out_ref[:, i * C : (i + 1) * C] = send_ref[y, i].astype(BF16)
        acc0 = [send_ref[y, i].astype(F32) for i in range(2)]
        for i in range(2):
            conv_ref[...] = acc0[i]
            for d in range(1, NY):
                other = lax.rem(y + d, NY)
                if i == 0:
                    remote(
                        send_ref.at[other], land_ref.at[other], y_send.at[other], y_recv.at[other], partner
                    ).wait_recv()
                conv_ref[...] += land_ref[other, i].astype(F32)
            out_ref[:, i * C : (i + 1) * C] = conv_ref[...].astype(BF16)
        for row in range(NY):

            @pl.when(row != y)
            def _(row=row):
                y_copy(row).wait_send()

    tasks = [(-1.0, send_tail), (-0.9, clear)]
    tasks += [(0.1 + 0.3 * i, lambda i=i: tables(4 * i)) for i in range(4)]
    tasks += [(2.0, mix), (2.2, forward_send), (2.6, lambda: shift_copies(0, 0)), (3.0, lambda: shift_copies(0, 4))]
    tasks += [(3.4 + 0.5 * i, lambda i=i: local_taps(0, 4 * i, 4 * i + 4, conv_ref, i == 0)) for i in range(4)]
    tasks += [(5.8, lambda: combine_x(0)), (11.0, gate)]
    when = 11.2
    for i, dz in enumerate(ROW_ORDER):
        when = max(when + 0.8, ROW_READY[dz] + 0.01 if i else 0.0)
        tasks.append((when, lambda dz=dz: project(dz)))
        if i:
            tasks.append((when + 0.001, lambda dz=ROW_ORDER[i - 1]: pass_on(dz)))
    tasks += [(now, lambda m=m, after=after: relay(m, after)) for now, m, after in ORDER]
    for _, task in sorted(tasks, key=lambda t: t[0]):
        task()

    acc_ref[...] = gg_ref[...] * mix_ref[0]
    end_state(near, acc_ref, 1)
    send_x(1)
    gg_ref[...] = gg_ref[...] * conv_ref[...]
    shift_copies(1, 0)
    shift_copies(1, 4)
    pass_on(ROW_ORDER[-1])
    combine_x(1)
    local_taps(1, 0, 16, acc_ref, True)
    combine_z(1)
    boundary(far, acc_ref)
    for j in range(3):
        value = gg_ref[...] if j == 0 else acc_ref[...] * mix_ref[3 - j]
        mix_ref[3 + j] = value
        tail_ref[1, 2 * j : 2 * j + 2, :] = value[0:2]
    copy = halo_copy(1, previous)
    copy.start()
    finish_output()
    copy.wait()
    inner = k < NZ * NX - 1
    for j in range(3):
        now = mix_ref[3 + j]
        one = jnp.where(inner, halo_ref[1, 2 * j : 2 * j + 1, :], 0.0)
        two = jnp.where(inner, halo_ref[1, 2 * j + 1 : 2 * j + 2, :], 0.0)
        ahead1 = jnp.where(rows == T - 1, one, pltpu.roll(now, T - 1, 0))
        ahead2 = jnp.where(rows == T - 1, two, jnp.where(rows == T - 2, one, pltpu.roll(now, T - 2, 0)))
        gf_ref[j] = (
            taps_ref[0, j : j + 1, :] * now + taps_ref[1, j : j + 1, :] * ahead1 + taps_ref[2, j : j + 1, :] * ahead2
        ).astype(BF16)
    for copy in pending:
        copy.wait_send()
    for which in range(2):
        for d in range(1, NZ):
            to = lax.rem(z + d, NZ)

            @pl.when((to > z) if which == 0 else (to < z))
            def _(which=which, d=d):
                z_copy(which, d).wait_send()


def per_device(featurized, short_taps, residues, decay_rates, w_out, grad_out):
    feats = featurized.transpose(1, 0, 2)
    vmem = pl.BlockSpec(memory_space=pltpu.VMEM)
    hbm = pl.BlockSpec(memory_space=pl.ANY)
    dma, V = pltpu.SemaphoreType.DMA, pltpu.VMEM
    block, gf = pl.pallas_call(
        kernel,
        out_shape=(jax.ShapeDtypeStruct((T, 2 * C), BF16), jax.ShapeDtypeStruct((3, T, C), BF16)),
        in_specs=[vmem, vmem, vmem, vmem, hbm, hbm],
        out_specs=(vmem, vmem),
        scratch_shapes=[
            V((NZ * NX, C, C), BF16),
            V((T, NZ * NX * C), BF16),
            V((MODES, T, C), F32),
            V((MODES, T, C), F32),
            V((T, C), F32),
            V((8, 2 * T, C), F32),
            V((6, T, C), F32),
            V((T, C), F32),
            V((T, C), F32),
            V((T, C), F32),
            V((2, 8, C), F32),
            V((2, 8, C), F32),
            V((8, MODES, C), F32),
            V((2, NX, MODES, C), F32),
            V((2, NZ, MODES, C), F32),
            V((NZ, NX, T, C), BF16),
            V((NZ, 2, T, C), BF16),
            V((NZ, 2, T, C), BF16),
            V((NY, 2, T, C), BF16),
            V((MODES, C), F32),
            dma((2,)), dma((len(ORDER),)), dma((len(ORDER),)), dma((2,)), dma((2,)),
            dma((2, NX)), dma((2, NX)), dma((2, NZ)), dma((2, NZ)),
            dma((NZ,)), dma((NZ,)), dma((NY,)), dma((NY,)),
        ],
        compiler_params=pltpu.CompilerParams(
            collective_id=0, has_side_effects=True, vmem_limit_bytes=48 * 1024 * 1024
        ),
    )(feats, short_taps, decay_rates.T, residues.T, w_out, grad_out)
    return (block, gf.transpose(1, 0, 2))


def solution(mesh):
    placed = (
        P("ctx", None, "fsdp"),
        P(None, None, "fsdp"),
        P("fsdp", None),
        P("fsdp", None),
        P("fsdp", "ctx"),
        P("ctx", None),
    )
    return jax.shard_map(
        per_device,
        mesh=mesh,
        in_specs=placed,
        out_specs=(P("ctx", "fsdp"), P("ctx", None, "fsdp")),
        check_vma=False,
    )
```

time: 288 us -> 79.7 us (0.28)
  the two profiles are of different devices: /device:TPU:1 before, /device:TPU:33 now
where the time goes in v2:
time: 79.7 us; the launch traced here: 79.3 us
  Pallas kernels  71.8 us (90%)
  local copies, waits for them, and re-layouts  6.89 us (9%)
    pallas_call x1, Pallas kernels, per_device(): pl.pallas_call(kernel, out_shape=(jax.ShapeDtypeStruct((T, 2 * C), BF16),...  71.8 us
    unnamed x14, local copies, waits for them, and re-layouts  6.89 us

profile of v2, /device:TPU:33, one launch (start us, length us, event | category | flops | bytes accessed | tf_op | source)
XLA Modules:
  0.0 79.3 jit_solution(6959889451461604274)
XLA Ops:
  0.6 0.0 copy-start
  0.6 1.6 %copy-done = bf16[128,8192]{1,0:T(8,128)(2,1)S(1)} copy-done((bf16[128,8192]{1,0:T(8,128)(2,1)S(1)}, bf16[128,8192]{1,0:T(8,128)(2,1)}, u32[]{:S(2)}) %copy-start) | copy-done | bytes 2097176
  2.2 0.0 copy-start.1
  2.2 0.9 %copy-done.1 = bf16[128,3,256]{2,0,1:T(8,128)(2,1)S(1)} copy-done((bf16[128,3,256]{2,0,1:T(8,128)(2,1)S(1)}, bf16[128,3,256]{2,0,1:T(8,128)(2,1)}, u32[]{:S(2)}) %copy-start.1) | copy-done | bytes 196632
  3.2 0.0 copy-start.2
  3.2 0.9 %copy-done.2 = bf16[256,256]{1,0:T(8,128)(2,1)S(1)} copy-done((bf16[256,256]{1,0:T(8,128)(2,1)S(1)}, bf16[256,256]{1,0:T(8,128)(2,1)}, u32[]{:S(2)}) %copy-start.2) | copy-done | bytes 131096
  4.1 0.0 copy-start.3
  4.1 0.7 copy-done.3
  4.8 0.0 copy-start.4
  4.8 0.7 copy-done.4
  5.5 0.0 copy-start.5
  5.5 0.7 copy-done.5
  6.2 71.8 %shard_map.77 = (bf16[128,512]{1,0:T(8,128)(2,1)S(1)}, bf16[3,128,256]{2,1,0:T(8,128)(2,1)S(1)}) custom-call(bf16[3,128,256]{2,1,0:T(8,128)(2,1)S(1)} %bitcast.4, f32[3,3,256]{2,1,0:T(4,128)S(1)} %copy-done.5, f32[16,256]{1,0:T(8,128)S(1)} %bitcast.6, f32[16,256]{1,0:T(8,128)S(1)} %bitcast.7, bf16[256,256]{1,0:T(8,128)(2,1)S(1)} %copy-done.2, ...), custom_call_target="tpu_custom_call" | custom-call | tf_op jit(solution)/shard_map/pallas_call | solution.py:408
  78.0 0.7 copy.10
  78.6 0.7 copy.11
Async XLA Ops:
  0.6 1.6 %copy-start = (bf16[128,8192]{1,0:T(8,128)(2,1)S(1)}, bf16[128,8192]{1,0:T(8,128)(2,1)}, u32[]{:S(2)}) copy-start(bf16[128,8192]{1,0:T(8,128)(2,1)} %go_ref.1) | copy-start | bytes 6291460
  2.2 0.9 %copy-start.1 = (bf16[128,3,256]{2,0,1:T(8,128)(2,1)S(1)}, bf16[128,3,256]{2,0,1:T(8,128)(2,1)}, u32[]{:S(2)}) copy-start(bf16[128,3,256]{2,0,1:T(8,128)(2,1)} %param.6) | copy-start | bytes 589828
  3.2 0.9 %copy-start.2 = (bf16[256,256]{1,0:T(8,128)(2,1)S(1)}, bf16[256,256]{1,0:T(8,128)(2,1)}, u32[]{:S(2)}) copy-start(bf16[256,256]{1,0:T(8,128)(2,1)} %w_ref.1) | copy-start | bytes 393220
  4.1 0.7 copy-start.3
  4.8 0.7 copy-start.4
  5.5 0.7 copy-start.5

commit v3 on v2

v3 whole, which is shorter than its diff:
```python
import jax
import jax.numpy as jnp
from jax import lax
from jax.experimental import pallas as pl
from jax.experimental.pallas import tpu as pltpu
from jax.sharding import PartitionSpec as P

T = 128
C = 256
MODES = 16
NZ, NX, NY = 8, 4, 8
F32 = jnp.float32
BF16 = jnp.bfloat16
MESH = pl.DeviceIdType.MESH

H = T // 2
CHAIN_UP = {0: (4, 3, 2, 1), 1: (3, 2, 1)}
CHAIN_DOWN = {0: (5, 6, 7), 1: (4, 5, 6, 7)}
PROJECT_ORDER = (4, 3, 5, 2, 6, 1, 7, 0)


def kernel(
    feats_in, taps_in, a_in, res_in, w_ref, go_ref, out_ref, gf_ref,
    feats_ref, taps_ref, a_ref, res_ref, w_all, go_all, hop_ref, near, far, h_ref, pad_ref, mix_ref, conv_ref, gg_ref,
    acc_ref, tail_ref, halo_ref, state_ref, x_states, z_states, weight_ref, gated_ref, part_ref, give_ref, take_ref,
    mine_ref, pair_ref, chain_ref, land_ref, final_ref, block_ref,
    own_sem, w_send, w_recv, halo_send, halo_recv, x_send, x_recv, z_send, z_recv,
    go_send, go_recv, hop_send, hop_recv, far_send, far_recv, share_send, share_recv,
    gated_send, gated_recv, give_send, give_recv, pair_send, pair_recv, y_send, y_recv, final_send, final_recv,
):
    f, k = lax.axis_index("fsdp"), lax.axis_index("ctx")
    y, core = f // 2, f % 2
    z, x = k // NX, k % NX

    def at(dz, dx):
        return lax.rem(z + dz + NZ, NZ) * NX + lax.rem(x + dx + NX, NX)

    def ctx(index):
        return {"fsdp": f, "ctx": index}

    def remote(src, dst, send, recv, device):
        return pltpu.make_async_remote_copy(
            src_ref=src, dst_ref=dst, send_sem=send, recv_sem=recv, device_id=device, device_id_type=MESH
        )

    following, previous = lax.rem(k + 1, NZ * NX), lax.rem(k + NZ * NX - 1, NZ * NX)
    partner = {"fsdp": y * 2 + 1 - core, "ctx": k}
    my_half = pl.ds(core * H, H)

    loads = [
        pltpu.make_async_copy(src, dst, own_sem.at[i])
        for i, (src, dst) in enumerate(
            [(feats_in, feats_ref), (a_in, a_ref), (res_in, res_ref), (taps_in, taps_ref), (w_ref, w_all.at[z])]
        )
    ]
    for load in loads:
        load.start()

    barrier = pltpu.get_barrier_semaphore()
    greeted = [{"fsdp": y * 2 + 1 - core, "ctx": at(0, d)} for d in range(NX)] + [ctx(at(0, d)) for d in range(1, NX)]
    greeted += [ctx(at(d, 0)) for d in range(1, NZ)] + [ctx(following), ctx(previous)]
    greeted += [{"fsdp": lax.rem(y + d, NY) * 2 + core, "ctx": k} for d in (1, NY - 1)]
    for device in greeted:
        pl.semaphore_signal(barrier, inc=1, device_id=device, device_id_type=MESH)
    pl.semaphore_wait(barrier, len(greeted))

    pending = []

    def go(copy):
        copy.start()
        pending.append(copy)

    def w_copy(distance, up, piece):
        block = lax.rem(z + (1 - distance if up else distance - 1) + NZ, NZ)
        span = pl.ds(piece * T, T)
        src = w_ref.at[span, :] if distance == 1 else w_all.at[block, span, :]
        slot = (0 if up else 1), distance - 1, piece
        return remote(src, w_all.at[block, span, :], w_send.at[slot], w_recv.at[slot], ctx(at(1 if up else -1, 0)))

    def w_relay(distance):
        for piece in range(2):
            for up in (True, False):
                if distance == NZ // 2 and piece != (0 if up else 1):
                    continue
                block = w_all.at[lax.rem(z + (-distance if up else distance) + NZ, NZ), pl.ds(piece * T, T), :]
                slot = (0 if up else 1), distance - 1, piece
                remote(block, block, w_send.at[slot], w_recv.at[slot], partner).wait_recv()
                last = distance + 1 == NZ // 2
                if distance < NZ // 2 and (not last or piece == (0 if up else 1)):
                    go(w_copy(distance + 1, up, piece))

    def strip(row, dx):
        return go_ref.at[my_half, pl.ds(pl.multiple_of((row * NX + lax.rem(x + dx + NX, NX)) * C, C), C)]

    def go_out(low, high):
        for row in range(low, high):
            for way, dx in enumerate((1, -1)):
                remote(
                    strip(row, dx), go_all.at[row, x, my_half, :], go_send.at[way], go_recv.at[way], ctx(at(0, dx))
                ).start()

    def go_hop():
        for i in range(NZ // 2):
            for way, dx in enumerate((1, -1)):
                remote(
                    strip(i + way * NZ // 2, 2), hop_ref.at[way, i], hop_send.at[way], hop_recv.at[way], ctx(at(0, dx))
                ).start()

    def all_rows(source):
        return go_all.at[:, source, my_half, :]

    def half_rows(way, source):
        return go_all.at[pl.ds(way * NZ // 2, NZ // 2), source, my_half, :]

    def from_x(dx):
        return lax.rem(x + dx + NX, NX)

    def hop_relay():
        for way, dx in enumerate((1, -1)):
            remote(hop_ref.at[way], hop_ref.at[way], hop_send.at[way], hop_recv.at[way], partner).wait_recv()
            go(remote(hop_ref.at[way], half_rows(way, from_x(-dx)), far_send.at[way], far_recv.at[way], ctx(at(0, dx))))

    def share(group):
        if group < 2:
            region = all_rows(from_x(-1 if group == 0 else 1))
            remote(region, region, go_send.at[group], go_recv.at[group], partner).wait_recv()
            go(remote(region, region, share_send.at[group], share_recv.at[group], partner))
        else:
            for way in range(2):
                region = half_rows(way, from_x(2))
                remote(region, region, far_send.at[way], far_recv.at[way], partner).wait_recv()
                go(remote(region, region, share_send.at[2 + way], share_recv.at[2 + way], partner))

    def shared():
        others = pl.ds((1 - core) * H, H)
        regions = [go_all.at[:, from_x(-1), others, :], go_all.at[:, from_x(1), others, :]]
        regions += [go_all.at[pl.ds(way * NZ // 2, NZ // 2), from_x(2), others, :] for way in range(2)]
        for i, region in enumerate(regions):
            remote(region, region, share_send.at[i], share_recv.at[i], partner).wait_recv()
        pltpu.make_async_copy(go_all.at[:, x], go_all.at[:, x], own_sem.at[5]).wait()

    def own_rows():
        for row in range(NZ):
            columns = pl.ds(pl.multiple_of((row * NX + x) * C, C), C)
            pltpu.make_async_copy(go_ref.at[:, columns], go_all.at[row, x], own_sem.at[5]).start()

    rows = lax.broadcasted_iota(jnp.int32, (T, 1), 0)
    steps = rows.astype(F32)

    def halo_copy(which, device):
        return remote(
            tail_ref.at[which], halo_ref.at[which], halo_send.at[which], halo_recv.at[which], ctx(device)
        )

    def send_tail():
        for j in range(3):
            last = feats_ref[j, T - 16 :, :].astype(F32)
            tail_ref[0, 2 * j : 2 * j + 2, :] = last[14:16]
        copy = halo_copy(0, following)
        copy.start()
        pending.append(copy)

    def tables(low):
        def body(n, c):
            a = a_ref[pl.ds(n, 1), :]
            scale = res_ref[pl.ds(n, 1), :] * jnp.sqrt(a)
            weight_ref[pl.ds(n, 1), :] = scale
            e = jnp.exp(-a * steps)
            near[n] = e
            far[n] = jnp.exp(-a * (T - 1 - steps))
            h_ref[...] += scale * e
            return c

        lax.fori_loop(low, low + 4, body, 0)

    def clear():
        h_ref[...] = jnp.zeros_like(h_ref)

    def end_state(table, signal_ref, which):
        def body(n, c):
            state_ref[which, pl.ds(n, 1), :] = jnp.sum(table[n] * signal_ref[...], axis=0, keepdims=True)
            return c

        lax.fori_loop(0, MODES, body, 0)

    def send_x(which):
        for d in range(1, NX):
            copy = remote(
                state_ref.at[which], x_states.at[which, x], x_send.at[which, d], x_recv.at[which, x], ctx(at(0, d))
            )
            copy.start()
            pending.append(copy)

    def mix():
        halo_copy(0, following).wait_recv()
        for j in range(3):
            now = feats_ref[j].astype(F32)
            one = jnp.where(k > 0, halo_ref[0, 2 * j + 1 : 2 * j + 2, :], 0.0)
            two = jnp.where(k > 0, halo_ref[0, 2 * j : 2 * j + 1, :], 0.0)
            back1 = jnp.where(rows == 0, one, pltpu.roll(now, 1, 0))
            back2 = jnp.where(rows == 0, two, jnp.where(rows == 1, one, pltpu.roll(now, 2, 0)))
            mix_ref[j] = (
                taps_ref[0, j : j + 1, :] * now + taps_ref[1, j : j + 1, :] * back1 + taps_ref[2, j : j + 1, :] * back2
            )
        acc_ref[...] = mix_ref[1] * mix_ref[2]

    def forward_send():
        end_state(far, acc_ref, 0)
        send_x(0)

    def shift_copies(which, low):
        value = acc_ref[...]
        for r in range(low, low + 4):
            if which == 0:
                pad_ref[r, :T, :] = jnp.zeros_like(value)
                pad_ref[r, T:, :] = jnp.where(rows >= r, pltpu.roll(value, r, 0), 0.0) if r else value
            else:
                pad_ref[r, T:, :] = jnp.zeros_like(value)
                pad_ref[r, :T, :] = jnp.where(rows < T - r, pltpu.roll(value, T - r, 0), 0.0) if r else value

    def local_taps(which, low, high, dst, begin):
        def body(q, total):
            for r in range(8):
                start = pl.multiple_of((T - 8 * q) if which == 0 else 8 * q, 8)
                total = total + h_ref[pl.ds(8 * q + r, 1), :] * pad_ref[r, pl.ds(start, T), :]
            return total

        first = jnp.zeros((T, C), F32) if begin else dst[...]
        dst[...] = lax.fori_loop(low, high, body, first)

    def combine_x(which):
        x_states[which, x] = state_ref[which]
        for d in range(1, NX):
            other = lax.rem(x + d, NX)
            remote(
                state_ref.at[which], x_states.at[which, other], x_send.at[which, d], x_recv.at[which, other], ctx(k)
            ).wait_recv()
        a = a_ref[...]
        entering, total = jnp.zeros_like(a), jnp.zeros_like(a)
        for j in range(NX):
            gap = (x - 1 - j) if which == 0 else (j - x - 1)
            reach = (NX - 1 - j) if which == 0 else j
            decay = jnp.exp(-a * (T * jnp.maximum(gap, 0)).astype(F32))
            state = x_states[which, j]
            entering = entering + jnp.where(gap >= 0, decay * state, 0.0)
            total = total + jnp.exp(-a * float(T * reach)) * state
        state_ref[2 + which] = entering
        state_ref[4 + which] = total
        for d in range(1, NZ):
            to = lax.rem(z + d, NZ)

            @pl.when((to > z) if which == 0 else (to < z))
            def _(d=d):
                z_copy(which, d).start()

    def z_copy(which, d):
        return remote(
            state_ref.at[4 + which], z_states.at[which, z], z_send.at[which, d], z_recv.at[which, z], ctx(at(d, 0))
        )

    def combine_z(which):
        a = a_ref[...]
        state_ref[6] = jnp.zeros_like(a)
        for d in range(1, NZ):
            other = lax.rem(z + d, NZ)

            @pl.when((other < z) if which == 0 else (other > z))
            def _(d=d, other=other):
                remote(
                    state_ref.at[4 + which],
                    z_states.at[which, other],
                    z_send.at[which, d],
                    z_recv.at[which, other],
                    ctx(at(d, 0)),
                ).wait_recv()
                gap = (z - 1 - other) if which == 0 else (other - z - 1)
                state_ref[6] += jnp.exp(-a * (NX * T * gap).astype(F32)) * z_states[which, other]

        inside = x if which == 0 else NX - 1 - x
        entering = state_ref[2 + which] + jnp.exp(-a * (T * inside).astype(F32)) * state_ref[6]
        state_ref[7] = weight_ref[...] * jnp.exp(-a) * entering

    def boundary(table, dst):
        def body(n, total):
            return total + table[n] * state_ref[7, pl.ds(n, 1), :]

        dst[...] = lax.fori_loop(0, MODES, body, dst[...])

    def gate():
        combine_z(0)
        boundary(near, conv_ref)
        gated_ref[x] = (mix_ref[0] * conv_ref[...]).astype(BF16)
        for d in range(1, NX):
            go(remote(gated_ref.at[x], gated_ref.at[x], gated_send.at[d], gated_recv.at[d], ctx(at(0, d))))

    def transpose_project():
        def body(row, c):
            part = lax.dot_general(
                go_all[row].reshape(NX * T, C), w_all[row], (((1,), (1,)), ((), ())), preferred_element_type=F32
            )
            part_ref[...] += part.reshape(NX, T, C)
            return c

        part_ref[...] = jnp.zeros_like(part_ref)
        lax.fori_loop(0, NZ, body, 0)
        for d in range(1, NX):
            to = lax.rem(x + d, NX)
            give_ref[d] = part_ref[to].astype(BF16)
            go(remote(give_ref.at[d], take_ref.at[d], give_send.at[d], give_recv.at[d], ctx(at(0, d))))

    def sum_gated():
        gg_ref[...] = part_ref[x]
        for d in range(1, NX):
            remote(give_ref.at[d], take_ref.at[d], give_send.at[d], give_recv.at[d], partner).wait_recv()
            gg_ref[...] += take_ref[d].astype(F32)

    def gated_arrived():
        for d in range(1, NX):
            source = from_x(-d)
            remote(
                gated_ref.at[source], gated_ref.at[source], gated_send.at[d], gated_recv.at[d], partner
            ).wait_recv()

    def target(e):
        return lax.rem(y + e, NY)

    def pair_copy(e):
        row = target(e)
        return remote(
            mine_ref.at[row, pl.ds((1 - core) * 2, 2)], pair_ref.at[row], pair_send.at[e], pair_recv.at[e], partner
        )

    def project(e):
        row = target(e)
        part = jnp.dot(gated_ref[...].reshape(NX * T, C), w_all[row], preferred_element_type=F32)
        mine_ref[row] = part.astype(BF16).reshape(NX, T, C)
        go(pair_copy(e))

    paired = set()

    def term(e, piece):
        if e not in paired:
            pair_copy(e).wait_recv()
            paired.add(e)
        row = target(e)
        return mine_ref[row, core * 2 + piece].astype(F32) + pair_ref[row, piece].astype(F32)

    def incoming(up, e, piece):
        slot = (0 if up else 1), e, piece
        landed = land_ref.at[slot]
        remote(landed, landed, y_send.at[0, 0], y_recv.at[slot], partner).wait_recv()
        return land_ref[slot].astype(F32)

    def chain(up, e, piece):
        total = term(e, piece)
        if e != (CHAIN_UP if up else CHAIN_DOWN)[piece][0]:
            total = total + incoming(up, e, piece)
        chain_ref[e, piece] = total.astype(BF16)
        there = (0 if up else 1), (e - 1 if up else (e + 1) % NY), piece
        to = {"fsdp": lax.rem(y + (1 if up else NY - 1), NY) * 2 + core, "ctx": k}
        go(remote(chain_ref.at[e, piece], land_ref.at[there], y_send.at[e, piece], y_recv.at[there], to))

    owner = x // 2

    def final_copy(piece):
        device = {"fsdp": y * 2 + owner, "ctx": z * NX + core * 2 + piece}
        return remote(final_ref.at[piece], block_ref.at[x % 2], final_send.at[piece], final_recv.at[x % 2], device)

    def stays(piece):
        return jnp.logical_and(owner == core, x % 2 == piece)

    def finish_chain(piece):
        total = term(0, piece) + incoming(True, 0, piece) + incoming(False, 0, piece)
        final_ref[piece] = total.astype(BF16)

        @pl.when(jnp.logical_not(stays(piece)))
        def _():
            final_copy(piece).start()

    def collect():
        for half in range(2):
            local = jnp.logical_and(owner == core, x % 2 == half)

            @pl.when(local)
            def _(half=half):
                out_ref[:, half * C : (half + 1) * C] = final_ref[half]

            @pl.when(jnp.logical_not(local))
            def _(half=half):
                remote(
                    final_ref.at[0], block_ref.at[half], final_send.at[0], final_recv.at[half], partner
                ).wait_recv()
                out_ref[:, half * C : (half + 1) * C] = block_ref[half]

    for piece in range(2):
        go(w_copy(1, True, piece))
        go(w_copy(1, False, piece))
    for load in loads[:4]:
        load.wait()
    send_tail()
    go_out(0, 3)
    own_rows()
    clear()
    for i in range(4):
        tables(4 * i)
    mix()
    forward_send()
    go_hop()
    go_out(3, NZ)
    w_relay(1)
    shift_copies(0, 0)
    shift_copies(0, 4)
    combine_x(0)
    local_taps(0, 0, 8, conv_ref, True)
    hop_relay()
    w_relay(2)
    local_taps(0, 8, 16, conv_ref, False)
    w_relay(3)
    gate()
    share(0)
    share(1)
    w_relay(4)
    share(2)
    loads[4].wait()
    shared()
    transpose_project()
    gated_arrived()
    for e in PROJECT_ORDER[:3]:
        project(e)
    chain(True, 4, 0)
    chain(False, 4, 1)
    chain(True, 3, 1)
    chain(False, 5, 0)
    sum_gated()
    acc_ref[...] = gg_ref[...] * mix_ref[0]
    end_state(near, acc_ref, 1)
    send_x(1)
    for e in PROJECT_ORDER[3:]:
        project(e)
    chain(True, 3, 0)
    chain(False, 5, 1)
    chain(True, 2, 1)
    chain(False, 6, 0)
    combine_x(1)
    gg_ref[...] = gg_ref[...] * conv_ref[...]
    shift_copies(1, 0)
    shift_copies(1, 4)
    chain(True, 2, 0)
    chain(False, 6, 1)
    chain(True, 1, 1)
    chain(False, 7, 0)
    local_taps(1, 0, 16, acc_ref, True)
    combine_z(1)
    boundary(far, acc_ref)
    for j in range(3):
        value = gg_ref[...] if j == 0 else acc_ref[...] * mix_ref[3 - j]
        mix_ref[3 + j] = value
        tail_ref[1, 2 * j : 2 * j + 2, :] = value[0:2]
    go(halo_copy(1, previous))
    chain(True, 1, 0)
    chain(False, 7, 1)
    finish_chain(1)
    finish_chain(0)
    halo_copy(1, previous).wait_recv()
    inner = k < NZ * NX - 1
    for j in range(3):
        now = mix_ref[3 + j]
        one = jnp.where(inner, halo_ref[1, 2 * j : 2 * j + 1, :], 0.0)
        two = jnp.where(inner, halo_ref[1, 2 * j + 1 : 2 * j + 2, :], 0.0)
        ahead1 = jnp.where(rows == T - 1, one, pltpu.roll(now, T - 1, 0))
        ahead2 = jnp.where(rows == T - 1, two, jnp.where(rows == T - 2, one, pltpu.roll(now, T - 2, 0)))
        gf_ref[j] = (
            taps_ref[0, j : j + 1, :] * now + taps_ref[1, j : j + 1, :] * ahead1 + taps_ref[2, j : j + 1, :] * ahead2
        ).astype(BF16)
    collect()
    for copy in pending:
        copy.wait_send()
    for way in range(2):
        remote(all_rows(x), all_rows(x), go_send.at[way], go_recv.at[way], partner).wait_send()
        remote(hop_ref.at[way], hop_ref.at[way], hop_send.at[way], hop_recv.at[way], partner).wait_send()
    for piece in range(2):

        @pl.when(jnp.logical_not(stays(piece)))
        def _(piece=piece):
            final_copy(piece).wait_send()

    for which in range(2):
        for d in range(1, NZ):
            to = lax.rem(z + d, NZ)

            @pl.when((to > z) if which == 0 else (to < z))
            def _(which=which, d=d):
                z_copy(which, d).wait_send()


def per_device(featurized, short_taps, residues, decay_rates, w_out, grad_out):
    feats = featurized.transpose(1, 0, 2)
    vmem = pl.BlockSpec(memory_space=pltpu.VMEM)
    hbm = pl.BlockSpec(memory_space=pl.ANY)
    dma, V = pltpu.SemaphoreType.DMA, pltpu.VMEM
    block, gf = pl.pallas_call(
        kernel,
        out_shape=(jax.ShapeDtypeStruct((T, 2 * C), BF16), jax.ShapeDtypeStruct((3, T, C), BF16)),
        in_specs=[hbm] * 6,
        out_specs=(vmem, vmem),
        scratch_shapes=[
            V((3, T, C), BF16),
            V((3, 3, C), F32),
            V((MODES, C), F32),
            V((MODES, C), F32),
            V((NZ, C, C), BF16),
            V((NZ, NX, T, C), BF16),
            V((2, NZ // 2, H, C), BF16),
            V((MODES, T, C), F32),
            V((MODES, T, C), F32),
            V((T, C), F32),
            V((8, 2 * T, C), F32),
            V((6, T, C), F32),
            V((T, C), F32),
            V((T, C), F32),
            V((T, C), F32),
            V((2, 8, C), F32),
            V((2, 8, C), F32),
            V((8, MODES, C), F32),
            V((2, NX, MODES, C), F32),
            V((2, NZ, MODES, C), F32),
            V((MODES, C), F32),
            V((NX, T, C), BF16),
            V((NX, T, C), F32),
            V((NX, T, C), BF16),
            V((NX, T, C), BF16),
            V((NY, NX, T, C), BF16),
            V((NY, 2, T, C), BF16),
            V((NY, 2, T, C), BF16),
            V((2, NY, 2, T, C), BF16),
            V((2, T, C), BF16),
            V((2, T, C), BF16),
            dma((6,)), dma((2, 4, 2)), dma((2, 4, 2)), dma((2,)), dma((2,)),
            dma((2, NX)), dma((2, NX)), dma((2, NZ)), dma((2, NZ)),
            dma((2,)), dma((2,)), dma((2,)), dma((2,)), dma((2,)), dma((2,)), dma((4,)), dma((4,)),
            dma((NX,)), dma((NX,)), dma((NX,)), dma((NX,)), dma((NY,)), dma((NY,)),
            dma((NY, 2)), dma((2, NY, 2)), dma((2,)), dma((2,)),
        ],
        compiler_params=pltpu.CompilerParams(
            collective_id=0, has_side_effects=True, vmem_limit_bytes=66600000
        ),
    )(feats, short_taps, decay_rates.T, residues.T, w_out, grad_out)
    return (block, gf.transpose(1, 0, 2))


def solution(mesh):
    placed = (
        P("ctx", None, "fsdp"),
        P(None, None, "fsdp"),
        P("fsdp", None),
        P("fsdp", None),
        P("fsdp", "ctx"),
        P("ctx", None),
    )
    return jax.shard_map(
        per_device,
        mesh=mesh,
        in_specs=placed,
        out_specs=(P("ctx", "fsdp"), P("ctx", None, "fsdp")),
        check_vma=False,
    )
```

time: 79.7 us -> 68.1 us (0.85)
  the two profiles are of different devices: /device:TPU:33 before, /device:TPU:1 now
where the time goes in v3:
time: 68.1 us; the launch traced here: 67.9 us
  Pallas kernels  64.1 us (94%)
  local copies, waits for them, and re-layouts  3.18 us (5%)
    pallas_call x1, Pallas kernels, per_device(): pl.pallas_call(kernel, out_shape=(jax.ShapeDtypeStruct((T, 2 * C), BF16),...  64.1 us
    unnamed x2, local copies, waits for them, and re-layouts  3.18 us

profile of v3, /device:TPU:1, one launch (start us, length us, event | category | flops | bytes accessed | tf_op | source)
XLA Modules:
  0.0 67.9 jit_solution(2356440974759575863)
XLA Ops:
  0.6 64.1 %shard_map.77 = (bf16[128,512]{1,0:T(8,128)(2,1)}, bf16[3,128,256]{2,1,0:T(8,128)(2,1)}) custom-call(bf16[3,128,256]{2,1,0:T(8,128)(2,1)} %bitcast.4, f32[3,3,256]{2,1,0:T(4,128)} %taps_in.1, f32[16,256]{1,0:T(8,128)} %bitcast.6, f32[16,256]{1,0:T(8,128)} %bitcast.7, bf16[256,256]{1,0:T(8,128)(2,1)} %w_ref.1, bf16[128,8192]{1,0:T(8,128)(2,1)} %go_ref.1), custom_call_target="tpu_custom_call" | custom-call | tf_op jit(solution)/shard_map/pallas_call | solution.py:501
  64.7 1.6 %copy.10 = bf16[128,512]{1,0:T(8,128)(2,1)} copy(bf16[128,512]{1,0:T(8,128)(2,1)} %get-tuple-element.8) | data formatting | bytes 262144
  66.3 1.6 %copy.11 = bf16[128,3,256]{2,0,1:T(8,128)(2,1)} copy(bf16[128,3,256]{2,0,1:T(8,128)(2,1)} %bitcast.5) | data formatting | bytes 393216

commit v4 on v3

--- a/solution.py
+++ b/solution.py
@@ -14,18 +14,19 @@
 MESH = pl.DeviceIdType.MESH
 
 H = T // 2
+PIECES = 4
 CHAIN_UP = {0: (4, 3, 2, 1), 1: (3, 2, 1)}
 CHAIN_DOWN = {0: (5, 6, 7), 1: (4, 5, 6, 7)}
 PROJECT_ORDER = (4, 3, 5, 2, 6, 1, 7, 0)
 
 
 def kernel(
-    feats_in, taps_in, a_in, res_in, w_ref, go_ref, out_ref, gf_ref,
-    feats_ref, taps_ref, a_ref, res_ref, w_all, go_all, hop_ref, near, far, h_ref, pad_ref, mix_ref, conv_ref, gg_ref,
+    feats_in, taps_in, a_in, res_in, w_ref, go_ref, out_hbm, gf_hbm,
+    feats_ref, taps_ref, a_ref, res_ref, w_all, go_all, near, far, h_ref, pad_ref, mix_ref, conv_ref, gg_ref,
     acc_ref, tail_ref, halo_ref, state_ref, x_states, z_states, weight_ref, gated_ref, part_ref, give_ref, take_ref,
-    mine_ref, pair_ref, chain_ref, land_ref, final_ref, block_ref,
+    mine_ref, pair_ref, chain_ref, land_ref, final_ref, block_ref, out_ref, gf_ref,
     own_sem, w_send, w_recv, halo_send, halo_recv, x_send, x_recv, z_send, z_recv,
-    go_send, go_recv, hop_send, hop_recv, far_send, far_recv, share_send, share_recv,
+    go_send, go_recv, ring_send, ring_recv, share_send, share_recv,
     gated_send, gated_recv, give_send, give_recv, pair_send, pair_recv, y_send, y_recv, final_send, final_recv,
 ):
     f, k = lax.axis_index("fsdp"), lax.axis_index("ctx")
@@ -72,77 +73,89 @@
 
     def w_copy(distance, up, piece):
         block = lax.rem(z + (1 - distance if up else distance - 1) + NZ, NZ)
-        span = pl.ds(piece * T, T)
+        span = pl.ds(piece * (C // PIECES), C // PIECES)
         src = w_ref.at[span, :] if distance == 1 else w_all.at[block, span, :]
         slot = (0 if up else 1), distance - 1, piece
         return remote(src, w_all.at[block, span, :], w_send.at[slot], w_recv.at[slot], ctx(at(1 if up else -1, 0)))
 
+    def farthest(up, piece):
+        return (piece < PIECES // 2) == up
+
     def w_relay(distance):
-        for piece in range(2):
+        for i in range(PIECES):
             for up in (True, False):
-                if distance == NZ // 2 and piece != (0 if up else 1):
+                piece = i if up else PIECES - 1 - i
+                if distance == NZ // 2 and not farthest(up, piece):
                     continue
-                block = w_all.at[lax.rem(z + (-distance if up else distance) + NZ, NZ), pl.ds(piece * T, T), :]
+                span = pl.ds(piece * (C // PIECES), C // PIECES)
+                block = w_all.at[lax.rem(z + (-distance if up else distance) + NZ, NZ), span, :]
                 slot = (0 if up else 1), distance - 1, piece
                 remote(block, block, w_send.at[slot], w_recv.at[slot], partner).wait_recv()
-                last = distance + 1 == NZ // 2
-                if distance < NZ // 2 and (not last or piece == (0 if up else 1)):
+                if distance + 1 < NZ // 2 or (distance + 1 == NZ // 2 and farthest(up, piece)):
                     go(w_copy(distance + 1, up, piece))
 
-    def strip(row, dx):
-        return go_ref.at[my_half, pl.ds(pl.multiple_of((row * NX + lax.rem(x + dx + NX, NX)) * C, C), C)]
-
-    def go_out(low, high):
-        for row in range(low, high):
-            for way, dx in enumerate((1, -1)):
-                remote(
-                    strip(row, dx), go_all.at[row, x, my_half, :], go_send.at[way], go_recv.at[way], ctx(at(0, dx))
-                ).start()
-
-    def go_hop():
-        for i in range(NZ // 2):
-            for way, dx in enumerate((1, -1)):
-                remote(
-                    strip(i + way * NZ // 2, 2), hop_ref.at[way, i], hop_send.at[way], hop_recv.at[way], ctx(at(0, dx))
-                ).start()
-
-    def all_rows(source):
-        return go_all.at[:, source, my_half, :]
-
-    def half_rows(way, source):
-        return go_all.at[pl.ds(way * NZ // 2, NZ // 2), source, my_half, :]
-
-    def from_x(dx):
-        return lax.rem(x + dx + NX, NX)
-
-    def hop_relay():
-        for way, dx in enumerate((1, -1)):
-            remote(hop_ref.at[way], hop_ref.at[way], hop_send.at[way], hop_recv.at[way], partner).wait_recv()
-            go(remote(hop_ref.at[way], half_rows(way, from_x(-dx)), far_send.at[way], far_recv.at[way], ctx(at(0, dx))))
-
-    def share(group):
-        if group < 2:
-            region = all_rows(from_x(-1 if group == 0 else 1))
-            remote(region, region, go_send.at[group], go_recv.at[group], partner).wait_recv()
-            go(remote(region, region, share_send.at[group], share_recv.at[group], partner))
-        else:
-            for way in range(2):
-                region = half_rows(way, from_x(2))
-                remote(region, region, far_send.at[way], far_recv.at[way], partner).wait_recv()
-                go(remote(region, region, share_send.at[2 + way], share_recv.at[2 + way], partner))
-
-    def shared():
-        others = pl.ds((1 - core) * H, H)
-        regions = [go_all.at[:, from_x(-1), others, :], go_all.at[:, from_x(1), others, :]]
-        regions += [go_all.at[pl.ds(way * NZ // 2, NZ // 2), from_x(2), others, :] for way in range(2)]
-        for i, region in enumerate(regions):
-            remote(region, region, share_send.at[i], share_recv.at[i], partner).wait_recv()
-        pltpu.make_async_copy(go_all.at[:, x], go_all.at[:, x], own_sem.at[5]).wait()
+    def strip_row(dy, i):
+        return lax.rem(y + dy + NY, NY // 2) + i * (NY // 2)
+
+    def go_out(i):
+        row = strip_row(0, i)
+        for d in (2, 1, 3):
+            strip = go_ref.at[my_half, pl.ds(pl.multiple_of((row * NX + lax.rem(x + d, NX)) * C, C), C)]
+            go(remote(strip, go_all.at[row, d, my_half, :], go_send.at[i, d], go_recv.at[i, d], ctx(at(0, d))))
 
     def own_rows():
         for row in range(NZ):
             columns = pl.ds(pl.multiple_of((row * NX + x) * C, C), C)
-            pltpu.make_async_copy(go_ref.at[:, columns], go_all.at[row, x], own_sem.at[5]).start()
+            pltpu.make_async_copy(go_ref.at[:, columns], go_all.at[row, 0], own_sem.at[5]).start()
+
+    def strips(dy, i, half):
+        return go_all.at[strip_row(dy, i), pl.ds(1, NX - 1), pl.ds(half * H, H), :]
+
+    def go_copy(dy, up, i):
+        region = strips(dy, i, core)
+        slot = (0 if up else 1), (0 if dy == 0 else 2), i
+        to = {"fsdp": lax.rem(y + (1 if up else NY - 1), NY) * 2 + core, "ctx": k}
+        return remote(region, region, ring_send.at[slot], ring_recv.at[slot], to)
+
+    def share_copy(dy, i, half):
+        region = strips(dy, i, half)
+        slot = dy + 1, i
+        return remote(region, region, share_send.at[slot], share_recv.at[slot], partner)
+
+    def go_first(i):
+        for d in range(1, NX):
+            landed = go_all.at[strip_row(0, i), d, my_half, :]
+            remote(landed, landed, go_send.at[i, d], go_recv.at[i, d], partner).wait_recv()
+        go(go_copy(0, True, i))
+        go(go_copy(0, False, i))
+        go(share_copy(0, i, core))
+
+    def go_near(i):
+        for up in (True, False):
+            dy = -1 if up else 1
+            region = strips(dy, i, core)
+            slot = (0 if up else 1), 0, i
+            remote(region, region, ring_send.at[slot], ring_recv.at[slot], partner).wait_recv()
+            if i == (0 if up else 1):
+                go(go_copy(dy, up, i))
+            go(share_copy(dy, i, core))
+
+    def go_far():
+        for up in (True, False):
+            i = 0 if up else 1
+            region = strips(2, i, core)
+            slot = (0 if up else 1), 2, i
+            remote(region, region, ring_send.at[slot], ring_recv.at[slot], partner).wait_recv()
+            go(share_copy(2, i, core))
+
+    def shared():
+        for dy in (0, -1, 1, 2):
+            for i in range(2):
+                share_copy(dy, i, 1 - core).wait_recv()
+        pltpu.make_async_copy(go_all.at[:, 0], go_all.at[:, 0], own_sem.at[5]).wait()
+
+    def from_x(dx):
+        return lax.rem(x + dx + NX, NX)
 
     rows = lax.broadcasted_iota(jnp.int32, (T, 1), 0)
     steps = rows.astype(F32)
@@ -304,12 +317,11 @@
         part_ref[...] = jnp.zeros_like(part_ref)
         lax.fori_loop(0, NZ, body, 0)
         for d in range(1, NX):
-            to = lax.rem(x + d, NX)
-            give_ref[d] = part_ref[to].astype(BF16)
-            go(remote(give_ref.at[d], take_ref.at[d], give_send.at[d], give_recv.at[d], ctx(at(0, d))))
+            give_ref[d] = part_ref[d].astype(BF16)
+            go(remote(give_ref.at[d], take_ref.at[d], give_send.at[d], give_recv.at[d], ctx(at(0, -d))))
 
     def sum_gated():
-        gg_ref[...] = part_ref[x]
+        gg_ref[...] = part_ref[0]
         for d in range(1, NX):
             remote(give_ref.at[d], take_ref.at[d], give_send.at[d], give_recv.at[d], partner).wait_recv()
             gg_ref[...] += take_ref[d].astype(F32)
@@ -392,51 +404,51 @@
                 ).wait_recv()
                 out_ref[:, half * C : (half + 1) * C] = block_ref[half]
 
-    for piece in range(2):
-        go(w_copy(1, True, piece))
-        go(w_copy(1, False, piece))
     for load in loads[:4]:
         load.wait()
     send_tail()
-    go_out(0, 3)
-    own_rows()
+    for piece in range(PIECES):
+        go(w_copy(1, True, piece))
+        go(w_copy(1, False, PIECES - 1 - piece))
+    go_out(0)
     clear()
     for i in range(4):
         tables(4 * i)
+    go_out(1)
+    own_rows()
     mix()
     forward_send()
-    go_hop()
-    go_out(3, NZ)
     w_relay(1)
+    go_first(0)
     shift_copies(0, 0)
     shift_copies(0, 4)
+    local_taps(0, 0, 8, conv_ref, True)
+    go_first(1)
     combine_x(0)
-    local_taps(0, 0, 8, conv_ref, True)
-    hop_relay()
     w_relay(2)
     local_taps(0, 8, 16, conv_ref, False)
+    go_near(0)
     w_relay(3)
+    go_near(1)
     gate()
-    share(0)
-    share(1)
     w_relay(4)
-    share(2)
     loads[4].wait()
+    go_far()
     shared()
     transpose_project()
     gated_arrived()
-    for e in PROJECT_ORDER[:3]:
+    for e in PROJECT_ORDER[:5]:
         project(e)
     chain(True, 4, 0)
     chain(False, 4, 1)
     chain(True, 3, 1)
     chain(False, 5, 0)
+    for e in PROJECT_ORDER[5:]:
+        project(e)
     sum_gated()
     acc_ref[...] = gg_ref[...] * mix_ref[0]
     end_state(near, acc_ref, 1)
     send_x(1)
-    for e in PROJECT_ORDER[3:]:
-        project(e)
     chain(True, 3, 0)
     chain(False, 5, 1)
     chain(True, 2, 1)
@@ -445,11 +457,12 @@
     gg_ref[...] = gg_ref[...] * conv_ref[...]
     shift_copies(1, 0)
     shift_copies(1, 4)
+    local_taps(1, 0, 8, acc_ref, True)
     chain(True, 2, 0)
     chain(False, 6, 1)
     chain(True, 1, 1)
     chain(False, 7, 0)
-    local_taps(1, 0, 16, acc_ref, True)
+    local_taps(1, 8, 16, acc_ref, False)
     combine_z(1)
     boundary(far, acc_ref)
     for j in range(3):
@@ -472,12 +485,13 @@
         gf_ref[j] = (
             taps_ref[0, j : j + 1, :] * now + taps_ref[1, j : j + 1, :] * ahead1 + taps_ref[2, j : j + 1, :] * ahead2
         ).astype(BF16)
+    write_gf = pltpu.make_async_copy(gf_ref, gf_hbm, own_sem.at[6])
+    write_gf.start()
     collect()
+    write_out = pltpu.make_async_copy(out_ref, out_hbm, own_sem.at[7])
+    write_out.start()
     for copy in pending:
         copy.wait_send()
-    for way in range(2):
-        remote(all_rows(x), all_rows(x), go_send.at[way], go_recv.at[way], partner).wait_send()
-        remote(hop_ref.at[way], hop_ref.at[way], hop_send.at[way], hop_recv.at[way], partner).wait_send()
     for piece in range(2):
 
         @pl.when(jnp.logical_not(stays(piece)))
@@ -492,17 +506,19 @@
             def _(which=which, d=d):
                 z_copy(which, d).wait_send()
 
+    write_gf.wait()
+    write_out.wait()
+
 
 def per_device(featurized, short_taps, residues, decay_rates, w_out, grad_out):
-    feats = featurized.transpose(1, 0, 2)
-    vmem = pl.BlockSpec(memory_space=pltpu.VMEM)
+    operands = (featurized.transpose(1, 0, 2), short_taps, decay_rates.T, residues.T, w_out, grad_out)
     hbm = pl.BlockSpec(memory_space=pl.ANY)
     dma, V = pltpu.SemaphoreType.DMA, pltpu.VMEM
     block, gf = pl.pallas_call(
         kernel,
         out_shape=(jax.ShapeDtypeStruct((T, 2 * C), BF16), jax.ShapeDtypeStruct((3, T, C), BF16)),
         in_specs=[hbm] * 6,
-        out_specs=(vmem, vmem),
+        out_specs=(hbm, hbm),
         scratch_shapes=[
             V((3, T, C), BF16),
             V((3, 3, C), F32),
@@ -510,7 +526,6 @@
             V((MODES, C), F32),
             V((NZ, C, C), BF16),
             V((NZ, NX, T, C), BF16),
-            V((2, NZ // 2, H, C), BF16),
             V((MODES, T, C), F32),
             V((MODES, T, C), F32),
             V((T, C), F32),
@@ -535,16 +550,18 @@
             V((2, NY, 2, T, C), BF16),
             V((2, T, C), BF16),
             V((2, T, C), BF16),
-            dma((6,)), dma((2, 4, 2)), dma((2, 4, 2)), dma((2,)), dma((2,)),
+            V((T, 2 * C), BF16),
+            V((3, T, C), BF16),
+            dma((8,)), dma((2, 4, PIECES)), dma((2, 4, PIECES)), dma((2,)), dma((2,)),
             dma((2, NX)), dma((2, NX)), dma((2, NZ)), dma((2, NZ)),
-            dma((2,)), dma((2,)), dma((2,)), dma((2,)), dma((2,)), dma((2,)), dma((4,)), dma((4,)),
+            dma((2, NX)), dma((2, NX)), dma((2, 3, 2)), dma((2, 3, 2)), dma((4, 2)), dma((4, 2)),
             dma((NX,)), dma((NX,)), dma((NX,)), dma((NX,)), dma((NY,)), dma((NY,)),
             dma((NY, 2)), dma((2, NY, 2)), dma((2,)), dma((2,)),
         ],
         compiler_params=pltpu.CompilerParams(
-            collective_id=0, has_side_effects=True, vmem_limit_bytes=66600000
+            collective_id=0, has_side_effects=True, vmem_limit_bytes=48000000
         ),
-    )(feats, short_taps, decay_rates.T, residues.T, w_out, grad_out)
+    )(*(pltpu.with_memory_space_constraint(v, pltpu.HBM) for v in operands))
     return (block, gf.transpose(1, 0, 2))
 
 

time: 68.1 us -> 63.2 us (0.928)
  Pallas kernels: 64.1 us -> 61.1 us
  local copies, waits for them, and re-layouts: 3.18 us -> 1.33 us
    pallas_call x1, Pallas kernels: 64.1 us -> 61.1 us  [per_device(): pl.pallas_call(kernel, out_shape=(jax.ShapeDtypeStruct((T, 2 * C), BF16),...]
    unnamed x2, local copies, waits for them, and re-layouts: 3.18 us -> 1.33 us
where the time goes in v4:
time: 63.2 us; the launch traced here: 63.1 us
  Pallas kernels  61.1 us (97%)
  local copies, waits for them, and re-layouts  1.33 us (2%)
  between operations  0.64 us (1%)
    pallas_call x1, Pallas kernels, per_device(): pl.pallas_call(kernel, out_shape=(jax.ShapeDtypeStruct((T, 2 * C), BF16),...  61.1 us
    unnamed x2, local copies, waits for them, and re-layouts  1.33 us

profile of v4, /device:TPU:1, one launch (start us, length us, event | category | flops | bytes accessed | tf_op | source)
XLA Modules:
  0.0 63.1 jit_solution(2017022655836582445)
XLA Ops:
  0.6 61.1 %shard_map.77 = (bf16[128,512]{1,0:T(8,128)(2,1)S(1)}, bf16[3,128,256]{2,1,0:T(8,128)(2,1)S(1)}) custom-call(bf16[3,128,256]{2,1,0:T(8,128)(2,1)} %bitcast.5, f32[3,3,256]{2,1,0:T(4,128)} %taps_in.1, f32[16,256]{1,0:T(8,128)} %bitcast.6, f32[16,256]{1,0:T(8,128)} %bitcast.7, bf16[256,256]{1,0:T(8,128)(2,1)} %w_ref.1, bf16[128,8192]{1,0:T(8,128)(2,1)} %go_ref.1), custom_call_target="tpu_custom_call" | custom-call | tf_op jit(solution)/shard_map/pallas_call | solution.py:517
  61.7 0.7 %copy.10 = bf16[128,512]{1,0:T(8,128)(2,1)} copy(bf16[128,512]{1,0:T(8,128)(2,1)S(1)} %get-tuple-element.8) | data formatting | bytes 262144
  62.4 0.7 %copy.11 = bf16[128,3,256]{2,0,1:T(8,128)(2,1)} copy(bf16[128,3,256]{2,0,1:T(8,128)(2,1)S(1)} %bitcast.4) | data formatting | bytes 393216

commit v5 on v4

--- a/solution.py
+++ b/solution.py
@@ -15,8 +15,8 @@
 
 H = T // 2
 PIECES = 4
-CHAIN_UP = {0: (4, 3, 2, 1), 1: (3, 2, 1)}
-CHAIN_DOWN = {0: (5, 6, 7), 1: (4, 5, 6, 7)}
+CHAIN_UP = {0: (4, 3, 2, 1), 1: (4, 3, 2, 1), 2: (3, 2, 1), 3: (3, 2, 1)}
+CHAIN_DOWN = {0: (5, 6, 7), 1: (5, 6, 7), 2: (4, 5, 6, 7), 3: (4, 5, 6, 7)}
 PROJECT_ORDER = (4, 3, 5, 2, 6, 1, 7, 0)
 
 
@@ -24,10 +24,10 @@
     feats_in, taps_in, a_in, res_in, w_ref, go_ref, out_hbm, gf_hbm,
     feats_ref, taps_ref, a_ref, res_ref, w_all, go_all, near, far, h_ref, pad_ref, mix_ref, conv_ref, gg_ref,
     acc_ref, tail_ref, halo_ref, state_ref, x_states, z_states, weight_ref, gated_ref, part_ref, give_ref, take_ref,
-    mine_ref, pair_ref, chain_ref, land_ref, final_ref, block_ref, out_ref, gf_ref,
+    mine_ref, pair_ref, chain_ref, land_ref, final_ref, out_ref, gf_ref,
     own_sem, w_send, w_recv, halo_send, halo_recv, x_send, x_recv, z_send, z_recv,
     go_send, go_recv, ring_send, ring_recv, share_send, share_recv,
-    gated_send, gated_recv, give_send, give_recv, pair_send, pair_recv, y_send, y_recv, final_send, final_recv,
+    gated_send, gated_recv, give_send, give_recv, pair_send, pair_recv, y_send, y_recv, final_recv,
 ):
     f, k = lax.axis_index("fsdp"), lax.axis_index("ctx")
     y, core = f // 2, f % 2
@@ -61,6 +61,9 @@
     greeted = [{"fsdp": y * 2 + 1 - core, "ctx": at(0, d)} for d in range(NX)] + [ctx(at(0, d)) for d in range(1, NX)]
     greeted += [ctx(at(d, 0)) for d in range(1, NZ)] + [ctx(following), ctx(previous)]
     greeted += [{"fsdp": lax.rem(y + d, NY) * 2 + core, "ctx": k} for d in (1, NY - 1)]
+    greeted += [
+        {"fsdp": lax.rem(y + d, NY) * 2 + x // 2, "ctx": z * NX + core * 2 + i} for d in (1, NY - 1) for i in range(2)
+    ]
     for device in greeted:
         pl.semaphore_signal(barrier, inc=1, device_id=device, device_id_type=MESH)
     pl.semaphore_wait(barrier, len(greeted))
@@ -350,59 +353,86 @@
 
     paired = set()
 
+    def rows_of(piece):
+        return pl.ds(piece % 2 * H, H)
+
     def term(e, piece):
         if e not in paired:
             pair_copy(e).wait_recv()
             paired.add(e)
-        row = target(e)
-        return mine_ref[row, core * 2 + piece].astype(F32) + pair_ref[row, piece].astype(F32)
-
-    def incoming(up, e, piece):
-        slot = (0 if up else 1), e, piece
-        landed = land_ref.at[slot]
-        remote(landed, landed, y_send.at[0, 0], y_recv.at[slot], partner).wait_recv()
-        return land_ref[slot].astype(F32)
+        row, span = target(e), rows_of(piece)
+        mine = mine_ref[row, core * 2 + piece // 2, span, :]
+        return mine.astype(F32) + pair_ref[row, piece // 2, span, :].astype(F32)
+
+    owner = x // 2
+
+    def owner_of(piece, dy):
+        return {"fsdp": lax.rem(y + dy + NY, NY) * 2 + owner, "ctx": z * NX + core * 2 + piece // 2}
+
+    def to_owner(piece, kind, e, dy):
+        there = kind, x % 2, rows_of(piece), slice(None)
+        return remote(
+            chain_ref.at[e, piece],
+            final_ref.at[there],
+            y_send.at[e, piece],
+            final_recv.at[kind, x % 2, piece % 2],
+            owner_of(piece, dy),
+        )
 
     def chain(up, e, piece):
         total = term(e, piece)
         if e != (CHAIN_UP if up else CHAIN_DOWN)[piece][0]:
-            total = total + incoming(up, e, piece)
+            slot = (0 if up else 1), e, piece
+            landed = land_ref.at[slot]
+            remote(landed, landed, y_send.at[0, 0], y_recv.at[slot], partner).wait_recv()
+            total = total + land_ref[slot].astype(F32)
         chain_ref[e, piece] = total.astype(BF16)
-        there = (0 if up else 1), (e - 1 if up else (e + 1) % NY), piece
+        if e == (1 if up else NY - 1):
+            go(to_owner(piece, 1 if up else 2, e, 1 if up else -1))
+            return
+        there = (0 if up else 1), (e - 1 if up else e + 1), piece
         to = {"fsdp": lax.rem(y + (1 if up else NY - 1), NY) * 2 + core, "ctx": k}
         go(remote(chain_ref.at[e, piece], land_ref.at[there], y_send.at[e, piece], y_recv.at[there], to))
 
-    owner = x // 2
-
-    def final_copy(piece):
-        device = {"fsdp": y * 2 + owner, "ctx": z * NX + core * 2 + piece}
-        return remote(final_ref.at[piece], block_ref.at[x % 2], final_send.at[piece], final_recv.at[x % 2], device)
+    def stage(n):
+        for i in range(2):
+            chain(True, 4 - n, i)
+            chain(False, 4 + n, 2 + i)
+        if n < 3:
+            for i in range(2):
+                chain(True, 3 - n, 2 + i)
+                chain(False, 5 + n, i)
 
     def stays(piece):
-        return jnp.logical_and(owner == core, x % 2 == piece)
-
-    def finish_chain(piece):
-        total = term(0, piece) + incoming(True, 0, piece) + incoming(False, 0, piece)
-        final_ref[piece] = total.astype(BF16)
-
-        @pl.when(jnp.logical_not(stays(piece)))
-        def _():
-            final_copy(piece).start()
+        return jnp.logical_and(owner == core, x % 2 == piece // 2)
+
+    def own_term():
+        for piece in range(4):
+            chain_ref[0, piece] = term(0, piece).astype(BF16)
+
+            @pl.when(jnp.logical_not(stays(piece)))
+            def _(piece=piece):
+                to_owner(piece, 0, 0, 0).start()
 
     def collect():
         for half in range(2):
             local = jnp.logical_and(owner == core, x % 2 == half)
-
-            @pl.when(local)
-            def _(half=half):
-                out_ref[:, half * C : (half + 1) * C] = final_ref[half]
-
-            @pl.when(jnp.logical_not(local))
-            def _(half=half):
-                remote(
-                    final_ref.at[0], block_ref.at[half], final_send.at[0], final_recv.at[half], partner
-                ).wait_recv()
-                out_ref[:, half * C : (half + 1) * C] = block_ref[half]
+            for part in range(2):
+                span, columns = rows_of(part), pl.ds(half * C, C)
+
+                @pl.when(local)
+                def _(half=half, part=part, span=span):
+                    final_ref[0, half, span, :] = chain_ref[0, 2 * half + part]
+
+                for kind in range(3):
+                    landed = final_ref.at[kind, half, span, :]
+                    arrived = remote(landed, landed, y_send.at[0, 0], final_recv.at[kind, half, part], partner)
+                    if kind:
+                        arrived.wait_recv()
+                    else:
+                        pl.when(jnp.logical_not(local))(arrived.wait_recv)
+                total = final_ref[0, half, span, :].astype(F32) + final_ref[1, half, span, :].astype(F32)
+                out_ref[span, columns] = (total + final_ref[2, half, span, :].astype(F32)).astype(BF16)
 
     for load in loads[:4]:
         load.wait()
@@ -439,29 +469,21 @@
     gated_arrived()
     for e in PROJECT_ORDER[:5]:
         project(e)
-    chain(True, 4, 0)
-    chain(False, 4, 1)
-    chain(True, 3, 1)
-    chain(False, 5, 0)
+    stage(0)
     for e in PROJECT_ORDER[5:]:
         project(e)
     sum_gated()
     acc_ref[...] = gg_ref[...] * mix_ref[0]
     end_state(near, acc_ref, 1)
     send_x(1)
-    chain(True, 3, 0)
-    chain(False, 5, 1)
-    chain(True, 2, 1)
-    chain(False, 6, 0)
+    stage(1)
+    own_term()
     combine_x(1)
     gg_ref[...] = gg_ref[...] * conv_ref[...]
     shift_copies(1, 0)
     shift_copies(1, 4)
     local_taps(1, 0, 8, acc_ref, True)
-    chain(True, 2, 0)
-    chain(False, 6, 1)
-    chain(True, 1, 1)
-    chain(False, 7, 0)
+    stage(2)
     local_taps(1, 8, 16, acc_ref, False)
     combine_z(1)
     boundary(far, acc_ref)
@@ -470,10 +492,7 @@
         mix_ref[3 + j] = value
         tail_ref[1, 2 * j : 2 * j + 2, :] = value[0:2]
     go(halo_copy(1, previous))
-    chain(True, 1, 0)
-    chain(False, 7, 1)
-    finish_chain(1)
-    finish_chain(0)
+    stage(3)
     halo_copy(1, previous).wait_recv()
     inner = k < NZ * NX - 1
     for j in range(3):
@@ -492,11 +511,11 @@
     write_out.start()
     for copy in pending:
         copy.wait_send()
-    for piece in range(2):
+    for piece in range(4):
 
         @pl.when(jnp.logical_not(stays(piece)))
         def _(piece=piece):
-            final_copy(piece).wait_send()
+            to_owner(piece, 0, 0, 0).wait_send()
 
     for which in range(2):
         for d in range(1, NZ):
@@ -546,17 +565,16 @@
             V((NX, T, C), BF16),
             V((NY, NX, T, C), BF16),
             V((NY, 2, T, C), BF16),
-            V((NY, 2, T, C), BF16),
-            V((2, NY, 2, T, C), BF16),
-            V((2, T, C), BF16),
-            V((2, T, C), BF16),
+            V((NY, 4, H, C), BF16),
+            V((2, NY, 4, H, C), BF16),
+            V((3, 2, T, C), BF16),
             V((T, 2 * C), BF16),
             V((3, T, C), BF16),
             dma((8,)), dma((2, 4, PIECES)), dma((2, 4, PIECES)), dma((2,)), dma((2,)),
             dma((2, NX)), dma((2, NX)), dma((2, NZ)), dma((2, NZ)),
             dma((2, NX)), dma((2, NX)), dma((2, 3, 2)), dma((2, 3, 2)), dma((4, 2)), dma((4, 2)),
             dma((NX,)), dma((NX,)), dma((NX,)), dma((NX,)), dma((NY,)), dma((NY,)),
-            dma((NY, 2)), dma((2, NY, 2)), dma((2,)), dma((2,)),
+            dma((NY, 4)), dma((2, NY, 4)), dma((3, 2, 2)),
         ],
         compiler_params=pltpu.CompilerParams(
             collective_id=0, has_side_effects=True, vmem_limit_bytes=48000000

time: 63.2 us -> 61.3 us (0.970)
  Pallas kernels: 61.1 us -> 59.2 us
    pallas_call x1, Pallas kernels: 61.1 us -> 59.2 us  [per_device(): pl.pallas_call(kernel, out_shape=(jax.ShapeDtypeStruct((T, 2 * C), BF16),...]
where the time goes in v5:
time: 61.3 us; the launch traced here: 61.2 us
  Pallas kernels  59.2 us (97%)
  local copies, waits for them, and re-layouts  1.33 us (2%)
  between operations  0.64 us (1%)
    pallas_call x1, Pallas kernels, per_device(): pl.pallas_call(kernel, out_shape=(jax.ShapeDtypeStruct((T, 2 * C), BF16),...  59.2 us
    unnamed x2, local copies, waits for them, and re-layouts  1.33 us

profile of v5, /device:TPU:1, one launch (start us, length us, event | category | flops | bytes accessed | tf_op | source)
XLA Modules:
  0.0 61.2 jit_solution(8069569845440026071)
XLA Ops:
  0.6 59.2 %shard_map.77 = (bf16[128,512]{1,0:T(8,128)(2,1)S(1)}, bf16[3,128,256]{2,1,0:T(8,128)(2,1)S(1)}) custom-call(bf16[3,128,256]{2,1,0:T(8,128)(2,1)} %bitcast.5, f32[3,3,256]{2,1,0:T(4,128)} %taps_in.1, f32[16,256]{1,0:T(8,128)} %bitcast.6, f32[16,256]{1,0:T(8,128)} %bitcast.7, bf16[256,256]{1,0:T(8,128)(2,1)} %w_ref.1, bf16[128,8192]{1,0:T(8,128)(2,1)} %go_ref.1), custom_call_target="tpu_custom_call" | custom-call | tf_op jit(solution)/shard_map/pallas_call | solution.py:536
  59.8 0.7 %copy.10 = bf16[128,512]{1,0:T(8,128)(2,1)} copy(bf16[128,512]{1,0:T(8,128)(2,1)S(1)} %get-tuple-element.8) | data formatting | bytes 262144
  60.5 0.7 %copy.11 = bf16[128,3,256]{2,0,1:T(8,128)(2,1)} copy(bf16[128,3,256]{2,0,1:T(8,128)(2,1)S(1)} %bitcast.4) | data formatting | bytes 393216

commit v6 on v5

--- a/solution.py
+++ b/solution.py
@@ -27,7 +27,7 @@
     mine_ref, pair_ref, chain_ref, land_ref, final_ref, out_ref, gf_ref,
     own_sem, w_send, w_recv, halo_send, halo_recv, x_send, x_recv, z_send, z_recv,
     go_send, go_recv, ring_send, ring_recv, share_send, share_recv,
-    gated_send, gated_recv, give_send, give_recv, pair_send, pair_recv, y_send, y_recv, final_recv,
+    gated_send, gated_recv, give_send, give_recv, pair_send, pair_recv, y_send, own_send, y_recv, final_recv,
 ):
     f, k = lax.axis_index("fsdp"), lax.axis_index("ctx")
     y, core = f // 2, f % 2
@@ -68,18 +68,15 @@
         pl.semaphore_signal(barrier, inc=1, device_id=device, device_id_type=MESH)
     pl.semaphore_wait(barrier, len(greeted))
 
-    pending = []
-
     def go(copy):
         copy.start()
-        pending.append(copy)
 
     def w_copy(distance, up, piece):
         block = lax.rem(z + (1 - distance if up else distance - 1) + NZ, NZ)
         span = pl.ds(piece * (C // PIECES), C // PIECES)
         src = w_ref.at[span, :] if distance == 1 else w_all.at[block, span, :]
         slot = (0 if up else 1), distance - 1, piece
-        return remote(src, w_all.at[block, span, :], w_send.at[slot], w_recv.at[slot], ctx(at(1 if up else -1, 0)))
+        return remote(src, w_all.at[block, span, :], w_send.at[0], w_recv.at[slot], ctx(at(1 if up else -1, 0)))
 
     def farthest(up, piece):
         return (piece < PIECES // 2) == up
@@ -93,7 +90,7 @@
                 span = pl.ds(piece * (C // PIECES), C // PIECES)
                 block = w_all.at[lax.rem(z + (-distance if up else distance) + NZ, NZ), span, :]
                 slot = (0 if up else 1), distance - 1, piece
-                remote(block, block, w_send.at[slot], w_recv.at[slot], partner).wait_recv()
+                remote(block, block, w_send.at[0], w_recv.at[slot], partner).wait_recv()
                 if distance + 1 < NZ // 2 or (distance + 1 == NZ // 2 and farthest(up, piece)):
                     go(w_copy(distance + 1, up, piece))
 
@@ -104,7 +101,7 @@
         row = strip_row(0, i)
         for d in (2, 1, 3):
             strip = go_ref.at[my_half, pl.ds(pl.multiple_of((row * NX + lax.rem(x + d, NX)) * C, C), C)]
-            go(remote(strip, go_all.at[row, d, my_half, :], go_send.at[i, d], go_recv.at[i, d], ctx(at(0, d))))
+            go(remote(strip, go_all.at[row, d, my_half, :], go_send.at[0], go_recv.at[i], ctx(at(0, d))))
 
     def own_rows():
         for row in range(NZ):
@@ -116,19 +113,17 @@
 
     def go_copy(dy, up, i):
         region = strips(dy, i, core)
-        slot = (0 if up else 1), (0 if dy == 0 else 2), i
+        slot = (0 if up else 1), (i if dy == 0 else 2)
         to = {"fsdp": lax.rem(y + (1 if up else NY - 1), NY) * 2 + core, "ctx": k}
-        return remote(region, region, ring_send.at[slot], ring_recv.at[slot], to)
+        return remote(region, region, ring_send.at[0], ring_recv.at[slot], to)
 
     def share_copy(dy, i, half):
         region = strips(dy, i, half)
-        slot = dy + 1, i
-        return remote(region, region, share_send.at[slot], share_recv.at[slot], partner)
+        return remote(region, region, share_send.at[0], share_recv.at[0], partner)
 
     def go_first(i):
-        for d in range(1, NX):
-            landed = go_all.at[strip_row(0, i), d, my_half, :]
-            remote(landed, landed, go_send.at[i, d], go_recv.at[i, d], partner).wait_recv()
+        landed = strips(0, i, core)
+        remote(landed, landed, go_send.at[0], go_recv.at[i], partner).wait_recv()
         go(go_copy(0, True, i))
         go(go_copy(0, False, i))
         go(share_copy(0, i, core))
@@ -137,8 +132,8 @@
         for up in (True, False):
             dy = -1 if up else 1
             region = strips(dy, i, core)
-            slot = (0 if up else 1), 0, i
-            remote(region, region, ring_send.at[slot], ring_recv.at[slot], partner).wait_recv()
+            slot = (0 if up else 1), i
+            remote(region, region, ring_send.at[0], ring_recv.at[slot], partner).wait_recv()
             if i == (0 if up else 1):
                 go(go_copy(dy, up, i))
             go(share_copy(dy, i, core))
@@ -147,14 +142,13 @@
         for up in (True, False):
             i = 0 if up else 1
             region = strips(2, i, core)
-            slot = (0 if up else 1), 2, i
-            remote(region, region, ring_send.at[slot], ring_recv.at[slot], partner).wait_recv()
+            slot = (0 if up else 1), 2
+            remote(region, region, ring_send.at[0], ring_recv.at[slot], partner).wait_recv()
             go(share_copy(2, i, core))
 
     def shared():
-        for dy in (0, -1, 1, 2):
-            for i in range(2):
-                share_copy(dy, i, 1 - core).wait_recv()
+        region = go_all.at[:, pl.ds(1, NX - 1), pl.ds((1 - core) * H, H), :]
+        remote(region, region, share_send.at[0], share_recv.at[0], partner).wait_recv()
         pltpu.make_async_copy(go_all.at[:, 0], go_all.at[:, 0], own_sem.at[5]).wait()
 
     def from_x(dx):
@@ -165,7 +159,7 @@
 
     def halo_copy(which, device):
         return remote(
-            tail_ref.at[which], halo_ref.at[which], halo_send.at[which], halo_recv.at[which], ctx(device)
+            tail_ref.at[which], halo_ref.at[which], halo_send.at[0], halo_recv.at[which], ctx(device)
         )
 
     def send_tail():
@@ -174,7 +168,6 @@
             tail_ref[0, 2 * j : 2 * j + 2, :] = last[14:16]
         copy = halo_copy(0, following)
         copy.start()
-        pending.append(copy)
 
     def tables(low):
         def body(n, c):
@@ -202,10 +195,9 @@
     def send_x(which):
         for d in range(1, NX):
             copy = remote(
-                state_ref.at[which], x_states.at[which, x], x_send.at[which, d], x_recv.at[which, x], ctx(at(0, d))
+                state_ref.at[which], x_states.at[which, x], x_send.at[which], x_recv.at[which, x], ctx(at(0, d))
             )
             copy.start()
-            pending.append(copy)
 
     def mix():
         halo_copy(0, following).wait_recv()
@@ -249,7 +241,7 @@
         for d in range(1, NX):
             other = lax.rem(x + d, NX)
             remote(
-                state_ref.at[which], x_states.at[which, other], x_send.at[which, d], x_recv.at[which, other], ctx(k)
+                state_ref.at[which], x_states.at[which, other], x_send.at[which], x_recv.at[which, other], ctx(k)
             ).wait_recv()
         a = a_ref[...]
         entering, total = jnp.zeros_like(a), jnp.zeros_like(a)
@@ -271,7 +263,7 @@
 
     def z_copy(which, d):
         return remote(
-            state_ref.at[4 + which], z_states.at[which, z], z_send.at[which, d], z_recv.at[which, z], ctx(at(d, 0))
+            state_ref.at[4 + which], z_states.at[which, z], z_send.at[0], z_recv.at[z], ctx(at(d, 0))
         )
 
     def combine_z(which):
@@ -285,8 +277,8 @@
                 remote(
                     state_ref.at[4 + which],
                     z_states.at[which, other],
-                    z_send.at[which, d],
-                    z_recv.at[which, other],
+                    z_send.at[0],
+                    z_recv.at[other],
                     ctx(at(d, 0)),
                 ).wait_recv()
                 gap = (z - 1 - other) if which == 0 else (other - z - 1)
@@ -307,7 +299,7 @@
         boundary(near, conv_ref)
         gated_ref[x] = (mix_ref[0] * conv_ref[...]).astype(BF16)
         for d in range(1, NX):
-            go(remote(gated_ref.at[x], gated_ref.at[x], gated_send.at[d], gated_recv.at[d], ctx(at(0, d))))
+            go(remote(gated_ref.at[x], gated_ref.at[x], gated_send.at[0], gated_recv.at[d], ctx(at(0, d))))
 
     def transpose_project():
         def body(row, c):
@@ -321,19 +313,20 @@
         lax.fori_loop(0, NZ, body, 0)
         for d in range(1, NX):
             give_ref[d] = part_ref[d].astype(BF16)
-            go(remote(give_ref.at[d], take_ref.at[d], give_send.at[d], give_recv.at[d], ctx(at(0, -d))))
+            go(remote(give_ref.at[d], take_ref.at[d], give_send.at[0], give_recv.at[0], ctx(at(0, -d))))
 
     def sum_gated():
         gg_ref[...] = part_ref[0]
+        taken = take_ref.at[pl.ds(1, NX - 1)]
+        remote(taken, taken, give_send.at[0], give_recv.at[0], partner).wait_recv()
         for d in range(1, NX):
-            remote(give_ref.at[d], take_ref.at[d], give_send.at[d], give_recv.at[d], partner).wait_recv()
             gg_ref[...] += take_ref[d].astype(F32)
 
     def gated_arrived():
         for d in range(1, NX):
             source = from_x(-d)
             remote(
-                gated_ref.at[source], gated_ref.at[source], gated_send.at[d], gated_recv.at[d], partner
+                gated_ref.at[source], gated_ref.at[source], gated_send.at[0], gated_recv.at[d], partner
             ).wait_recv()
 
     def target(e):
@@ -342,7 +335,7 @@
     def pair_copy(e):
         row = target(e)
         return remote(
-            mine_ref.at[row, pl.ds((1 - core) * 2, 2)], pair_ref.at[row], pair_send.at[e], pair_recv.at[e], partner
+            mine_ref.at[row, pl.ds((1 - core) * 2, 2)], pair_ref.at[row], pair_send.at[0], pair_recv.at[e], partner
         )
 
     def project(e):
@@ -374,7 +367,7 @@
         return remote(
             chain_ref.at[e, piece],
             final_ref.at[there],
-            y_send.at[e, piece],
+            y_send.at[0] if kind else own_send.at[piece],
             final_recv.at[kind, x % 2, piece % 2],
             owner_of(piece, dy),
         )
@@ -384,7 +377,7 @@
         if e != (CHAIN_UP if up else CHAIN_DOWN)[piece][0]:
             slot = (0 if up else 1), e, piece
             landed = land_ref.at[slot]
-            remote(landed, landed, y_send.at[0, 0], y_recv.at[slot], partner).wait_recv()
+            remote(landed, landed, y_send.at[0], y_recv.at[slot[0], e - (1 if up else 5), piece], partner).wait_recv()
             total = total + land_ref[slot].astype(F32)
         chain_ref[e, piece] = total.astype(BF16)
         if e == (1 if up else NY - 1):
@@ -392,7 +385,7 @@
             return
         there = (0 if up else 1), (e - 1 if up else e + 1), piece
         to = {"fsdp": lax.rem(y + (1 if up else NY - 1), NY) * 2 + core, "ctx": k}
-        go(remote(chain_ref.at[e, piece], land_ref.at[there], y_send.at[e, piece], y_recv.at[there], to))
+        go(remote(chain_ref.at[e, piece], land_ref.at[there], y_send.at[0], y_recv.at[there[0], there[1] - (1 if up else 5), piece], to))
 
     def stage(n):
         for i in range(2):
@@ -426,7 +419,7 @@
 
                 for kind in range(3):
                     landed = final_ref.at[kind, half, span, :]
-                    arrived = remote(landed, landed, y_send.at[0, 0], final_recv.at[kind, half, part], partner)
+                    arrived = remote(landed, landed, y_send.at[0], final_recv.at[kind, half, part], partner)
                     if kind:
                         arrived.wait_recv()
                     else:
@@ -509,21 +502,27 @@
     collect()
     write_out = pltpu.make_async_copy(out_ref, out_hbm, own_sem.at[7])
     write_out.start()
-    for copy in pending:
-        copy.wait_send()
+    rows_sent = go_all.at[pl.ds(0, 6), pl.ds(1, NX - 1), my_half, :]
+    for sent, semaphore in [
+        (w_all.at[pl.ds(0, NZ - 1)], w_send.at[0]),
+        (go_all.at[pl.ds(0, 6), 1, my_half, :], go_send.at[0]),
+        (rows_sent, ring_send.at[0]),
+        (go_all.at[:, pl.ds(1, NX - 1), my_half, :], share_send.at[0]),
+        (tail_ref, halo_send.at[0]),
+        (x_states.at[0, pl.ds(0, NX - 1)], x_send.at[0]),
+        (x_states.at[1, pl.ds(0, NX - 1)], x_send.at[1]),
+        (z_states.at[0, pl.ds(0, NZ - 1)], z_send.at[0]),
+        (gated_ref.at[pl.ds(0, NX - 1)], gated_send.at[0]),
+        (give_ref.at[pl.ds(1, NX - 1)], give_send.at[0]),
+        (pair_ref, pair_send.at[0]),
+        (chain_ref.at[pl.ds(1, NY - 1)], y_send.at[0]),
+    ]:
+        remote(sent, sent, semaphore, own_sem.at[0], partner).wait_send()
     for piece in range(4):
 
         @pl.when(jnp.logical_not(stays(piece)))
         def _(piece=piece):
             to_owner(piece, 0, 0, 0).wait_send()
-
-    for which in range(2):
-        for d in range(1, NZ):
-            to = lax.rem(z + d, NZ)
-
-            @pl.when((to > z) if which == 0 else (to < z))
-            def _(which=which, d=d):
-                z_copy(which, d).wait_send()
 
     write_gf.wait()
     write_out.wait()
@@ -570,11 +569,11 @@
             V((3, 2, T, C), BF16),
             V((T, 2 * C), BF16),
             V((3, T, C), BF16),
-            dma((8,)), dma((2, 4, PIECES)), dma((2, 4, PIECES)), dma((2,)), dma((2,)),
-            dma((2, NX)), dma((2, NX)), dma((2, NZ)), dma((2, NZ)),
-            dma((2, NX)), dma((2, NX)), dma((2, 3, 2)), dma((2, 3, 2)), dma((4, 2)), dma((4, 2)),
-            dma((NX,)), dma((NX,)), dma((NX,)), dma((NX,)), dma((NY,)), dma((NY,)),
-            dma((NY, 4)), dma((2, NY, 4)), dma((3, 2, 2)),
+            dma((8,)), dma((1,)), dma((2, 4, PIECES)), dma((1,)), dma((2,)),
+            dma((2,)), dma((2, NX)), dma((1,)), dma((NZ,)),
+            dma((1,)), dma((2,)), dma((1,)), dma((2, 3)), dma((1,)), dma((1,)),
+            dma((1,)), dma((NX,)), dma((1,)), dma((1,)), dma((1,)), dma((NY,)),
+            dma((1,)), dma((4,)), dma((2, 3, 4)), dma((3, 2, 2)),
         ],
         compiler_params=pltpu.CompilerParams(
             collective_id=0, has_side_effects=True, vmem_limit_bytes=48000000

time: 61.3 us -> 59.4 us (0.969)
  Pallas kernels: 59.2 us -> 57.3 us
    pallas_call x1, Pallas kernels: 59.2 us -> 57.3 us  [per_device(): pl.pallas_call(kernel, out_shape=(jax.ShapeDtypeStruct((T, 2 * C), BF16),...]
where the time goes in v6:
time: 59.4 us; the launch traced here: 59.3 us
  Pallas kernels  57.3 us (96%)
  local copies, waits for them, and re-layouts  1.33 us (2%)
  between operations  0.64 us (1%)
    pallas_call x1, Pallas kernels, per_device(): pl.pallas_call(kernel, out_shape=(jax.ShapeDtypeStruct((T, 2 * C), BF16),...  57.3 us
    unnamed x2, local copies, waits for them, and re-layouts  1.33 us

profile of v6, /device:TPU:1, one launch (start us, length us, event | category | flops | bytes accessed | tf_op | source)
XLA Modules:
  0.0 59.3 jit_solution(14945111937595232144)
XLA Ops:
  0.6 57.3 %shard_map.77 = (bf16[128,512]{1,0:T(8,128)(2,1)S(1)}, bf16[3,128,256]{2,1,0:T(8,128)(2,1)S(1)}) custom-call(bf16[3,128,256]{2,1,0:T(8,128)(2,1)} %bitcast.5, f32[3,3,256]{2,1,0:T(4,128)} %taps_in.1, f32[16,256]{1,0:T(8,128)} %bitcast.6, f32[16,256]{1,0:T(8,128)} %bitcast.7, bf16[256,256]{1,0:T(8,128)(2,1)} %w_ref.1, bf16[128,8192]{1,0:T(8,128)(2,1)} %go_ref.1), custom_call_target="tpu_custom_call" | custom-call | tf_op jit(solution)/shard_map/pallas_call | solution.py:535
  58.0 0.7 %copy.10 = bf16[128,512]{1,0:T(8,128)(2,1)} copy(bf16[128,512]{1,0:T(8,128)(2,1)S(1)} %get-tuple-element.8) | data formatting | bytes 262144
  58.6 0.7 %copy.11 = bf16[128,3,256]{2,0,1:T(8,128)(2,1)} copy(bf16[128,3,256]{2,0,1:T(8,128)(2,1)S(1)} %bitcast.4) | data formatting | bytes 393216

commit v7 on v6

--- a/solution.py
+++ b/solution.py
@@ -21,10 +21,10 @@
 
 
 def kernel(
-    feats_in, taps_in, a_in, res_in, w_ref, go_ref, out_hbm, gf_hbm,
+    feats_in, taps_in, a_in, res_in, w_ref, go_ref, out_ref, gf_ref,
     feats_ref, taps_ref, a_ref, res_ref, w_all, go_all, near, far, h_ref, pad_ref, mix_ref, conv_ref, gg_ref,
     acc_ref, tail_ref, halo_ref, state_ref, x_states, z_states, weight_ref, gated_ref, part_ref, give_ref, take_ref,
-    mine_ref, pair_ref, chain_ref, land_ref, final_ref, out_ref, gf_ref,
+    mine_ref, pair_ref, chain_ref, land_ref, final_ref,
     own_sem, w_send, w_recv, halo_send, halo_recv, x_send, x_recv, z_send, z_recv,
     go_send, go_recv, ring_send, ring_recv, share_send, share_recv,
     gated_send, gated_recv, give_send, give_recv, pair_send, pair_recv, y_send, own_send, y_recv, final_recv,
@@ -81,8 +81,8 @@
     def farthest(up, piece):
         return (piece < PIECES // 2) == up
 
-    def w_relay(distance):
-        for i in range(PIECES):
+    def w_relay(distance, pieces=range(PIECES)):
+        for i in pieces:
             for up in (True, False):
                 piece = i if up else PIECES - 1 - i
                 if distance == NZ // 2 and not farthest(up, piece):
@@ -119,7 +119,7 @@
 
     def share_copy(dy, i, half):
         region = strips(dy, i, half)
-        return remote(region, region, share_send.at[0], share_recv.at[0], partner)
+        return remote(region, region, share_send.at[0], share_recv.at[dy + 1, i], partner)
 
     def go_first(i):
         landed = strips(0, i, core)
@@ -145,11 +145,6 @@
             slot = (0 if up else 1), 2
             remote(region, region, ring_send.at[0], ring_recv.at[slot], partner).wait_recv()
             go(share_copy(2, i, core))
-
-    def shared():
-        region = go_all.at[:, pl.ds(1, NX - 1), pl.ds((1 - core) * H, H), :]
-        remote(region, region, share_send.at[0], share_recv.at[0], partner).wait_recv()
-        pltpu.make_async_copy(go_all.at[:, 0], go_all.at[:, 0], own_sem.at[5]).wait()
 
     def from_x(dx):
         return lax.rem(x + dx + NX, NX)
@@ -301,16 +296,21 @@
         for d in range(1, NX):
             go(remote(gated_ref.at[x], gated_ref.at[x], gated_send.at[0], gated_recv.at[d], ctx(at(0, d))))
 
-    def transpose_project():
-        def body(row, c):
+    def transpose_project(dy):
+        for i in range(2):
+            share_copy(dy, i, 1 - core).wait_recv()
+
+        def body(i, c):
+            row = strip_row(dy, i)
             part = lax.dot_general(
                 go_all[row].reshape(NX * T, C), w_all[row], (((1,), (1,)), ((), ())), preferred_element_type=F32
             )
             part_ref[...] += part.reshape(NX, T, C)
             return c
 
-        part_ref[...] = jnp.zeros_like(part_ref)
-        lax.fori_loop(0, NZ, body, 0)
+        lax.fori_loop(0, 2, body, 0)
+
+    def give():
         for d in range(1, NX):
             give_ref[d] = part_ref[d].astype(BF16)
             go(remote(give_ref.at[d], take_ref.at[d], give_send.at[0], give_recv.at[0], ctx(at(0, -d))))
@@ -451,14 +451,19 @@
     w_relay(2)
     local_taps(0, 8, 16, conv_ref, False)
     go_near(0)
-    w_relay(3)
+    w_relay(3, range(PIECES // 2))
     go_near(1)
+    w_relay(3, range(PIECES // 2, PIECES))
     gate()
     w_relay(4)
     loads[4].wait()
+    pltpu.make_async_copy(go_all.at[:, 0], go_all.at[:, 0], own_sem.at[5]).wait()
+    part_ref[...] = jnp.zeros_like(part_ref)
+    for dy in (0, -1, 1):
+        transpose_project(dy)
     go_far()
-    shared()
-    transpose_project()
+    transpose_project(2)
+    give()
     gated_arrived()
     for e in PROJECT_ORDER[:5]:
         project(e)
@@ -497,11 +502,7 @@
         gf_ref[j] = (
             taps_ref[0, j : j + 1, :] * now + taps_ref[1, j : j + 1, :] * ahead1 + taps_ref[2, j : j + 1, :] * ahead2
         ).astype(BF16)
-    write_gf = pltpu.make_async_copy(gf_ref, gf_hbm, own_sem.at[6])
-    write_gf.start()
     collect()
-    write_out = pltpu.make_async_copy(out_ref, out_hbm, own_sem.at[7])
-    write_out.start()
     rows_sent = go_all.at[pl.ds(0, 6), pl.ds(1, NX - 1), my_half, :]
     for sent, semaphore in [
         (w_all.at[pl.ds(0, NZ - 1)], w_send.at[0]),
@@ -524,9 +525,6 @@
         def _(piece=piece):
             to_owner(piece, 0, 0, 0).wait_send()
 
-    write_gf.wait()
-    write_out.wait()
-
 
 def per_device(featurized, short_taps, residues, decay_rates, w_out, grad_out):
     operands = (featurized.transpose(1, 0, 2), short_taps, decay_rates.T, residues.T, w_out, grad_out)
@@ -536,7 +534,7 @@
         kernel,
         out_shape=(jax.ShapeDtypeStruct((T, 2 * C), BF16), jax.ShapeDtypeStruct((3, T, C), BF16)),
         in_specs=[hbm] * 6,
-        out_specs=(hbm, hbm),
+        out_specs=(pl.BlockSpec(memory_space=pltpu.VMEM),) * 2,
         scratch_shapes=[
             V((3, T, C), BF16),
             V((3, 3, C), F32),
@@ -567,11 +565,9 @@
             V((NY, 4, H, C), BF16),
             V((2, NY, 4, H, C), BF16),
             V((3, 2, T, C), BF16),
-            V((T, 2 * C), BF16),
-            V((3, T, C), BF16),
-            dma((8,)), dma((1,)), dma((2, 4, PIECES)), dma((1,)), dma((2,)),
+            dma((6,)), dma((1,)), dma((2, 4, PIECES)), dma((1,)), dma((2,)),
             dma((2,)), dma((2, NX)), dma((1,)), dma((NZ,)),
-            dma((1,)), dma((2,)), dma((1,)), dma((2, 3)), dma((1,)), dma((1,)),
+            dma((1,)), dma((2,)), dma((1,)), dma((2, 3)), dma((1,)), dma((4, 2)),
             dma((1,)), dma((NX,)), dma((1,)), dma((1,)), dma((1,)), dma((NY,)),
             dma((1,)), dma((4,)), dma((2, 3, 4)), dma((3, 2, 2)),
         ],

time: 59.4 us -> 57.8 us (0.973)
  Pallas kernels: 57.3 us -> 55.8 us
    pallas_call x1, Pallas kernels: 57.3 us -> 55.8 us  [per_device(): pl.pallas_call(kernel, out_shape=(jax.ShapeDtypeStruct((T, 2 * C), BF16),...]
where the time goes in v7:
time: 57.8 us; the launch traced here: 57.7 us
  Pallas kernels  55.8 us (97%)
  local copies, waits for them, and re-layouts  1.33 us (2%)
  between operations  0.64 us (1%)
    pallas_call x1, Pallas kernels, per_device(): pl.pallas_call(kernel, out_shape=(jax.ShapeDtypeStruct((T, 2 * C), BF16),...  55.8 us
    unnamed x2, local copies, waits for them, and re-layouts  1.33 us

profile of v7, /device:TPU:1, one launch (start us, length us, event | category | flops | bytes accessed | tf_op | source)
XLA Modules:
  0.0 57.7 jit_solution(15703034483023650257)
XLA Ops:
  0.6 55.8 %shard_map.77 = (bf16[128,512]{1,0:T(8,128)(2,1)S(1)}, bf16[3,128,256]{2,1,0:T(8,128)(2,1)S(1)}) custom-call(bf16[3,128,256]{2,1,0:T(8,128)(2,1)} %bitcast.5, f32[3,3,256]{2,1,0:T(4,128)} %taps_in.1, f32[16,256]{1,0:T(8,128)} %bitcast.6, f32[16,256]{1,0:T(8,128)} %bitcast.7, bf16[256,256]{1,0:T(8,128)(2,1)} %w_ref.1, bf16[128,8192]{1,0:T(8,128)(2,1)} %go_ref.1), custom_call_target="tpu_custom_call" | custom-call | tf_op jit(solution)/shard_map/pallas_call | solution.py:533
  56.4 0.7 %copy.10 = bf16[128,512]{1,0:T(8,128)(2,1)} copy(bf16[128,512]{1,0:T(8,128)(2,1)S(1)} %get-tuple-element.8) | data formatting | bytes 262144
  57.1 0.7 %copy.11 = bf16[128,3,256]{2,0,1:T(8,128)(2,1)} copy(bf16[128,3,256]{2,0,1:T(8,128)(2,1)S(1)} %bitcast.4) | data formatting | bytes 393216

commit v8 on v7

--- a/solution.py
+++ b/solution.py
@@ -188,7 +188,7 @@
         lax.fori_loop(0, MODES, body, 0)
 
     def send_x(which):
-        for d in range(1, NX):
+        for d in (2, 1, 3):
             copy = remote(
                 state_ref.at[which], x_states.at[which, x], x_send.at[which], x_recv.at[which, x], ctx(at(0, d))
             )
@@ -293,7 +293,7 @@
         combine_z(0)
         boundary(near, conv_ref)
         gated_ref[x] = (mix_ref[0] * conv_ref[...]).astype(BF16)
-        for d in range(1, NX):
+        for d in (2, 1, 3):
             go(remote(gated_ref.at[x], gated_ref.at[x], gated_send.at[0], gated_recv.at[d], ctx(at(0, d))))
 
     def transpose_project(dy):
@@ -311,7 +311,7 @@
         lax.fori_loop(0, 2, body, 0)
 
     def give():
-        for d in range(1, NX):
+        for d in (2, 1, 3):
             give_ref[d] = part_ref[d].astype(BF16)
             go(remote(give_ref.at[d], take_ref.at[d], give_send.at[0], give_recv.at[0], ctx(at(0, -d))))
 

time: 57.8 us -> 58 us (level)
  no operation moved by 1% of the time
where the time goes in v8:
time: 58 us; the launch traced here: 57.9 us
  Pallas kernels  55.9 us (96%)
  local copies, waits for them, and re-layouts  1.33 us (2%)
  between operations  0.64 us (1%)
    pallas_call x1, Pallas kernels, per_device(): pl.pallas_call(kernel, out_shape=(jax.ShapeDtypeStruct((T, 2 * C), BF16),...  55.9 us
    unnamed x2, local copies, waits for them, and re-layouts  1.33 us

profile of v8, /device:TPU:1, one launch (start us, length us, event | category | flops | bytes accessed | tf_op | source)
XLA Modules:
  0.0 57.9 jit_solution(15231847284874024030)
XLA Ops:
  0.6 55.9 %shard_map.77 = (bf16[128,512]{1,0:T(8,128)(2,1)S(1)}, bf16[3,128,256]{2,1,0:T(8,128)(2,1)S(1)}) custom-call(bf16[3,128,256]{2,1,0:T(8,128)(2,1)} %bitcast.5, f32[3,3,256]{2,1,0:T(4,128)} %taps_in.1, f32[16,256]{1,0:T(8,128)} %bitcast.6, f32[16,256]{1,0:T(8,128)} %bitcast.7, bf16[256,256]{1,0:T(8,128)(2,1)} %w_ref.1, bf16[128,8192]{1,0:T(8,128)(2,1)} %go_ref.1), custom_call_target="tpu_custom_call" | custom-call | tf_op jit(solution)/shard_map/pallas_call | solution.py:533
  56.6 0.7 %copy.10 = bf16[128,512]{1,0:T(8,128)(2,1)} copy(bf16[128,512]{1,0:T(8,128)(2,1)S(1)} %get-tuple-element.8) | data formatting | bytes 262144
  57.2 0.7 %copy.11 = bf16[128,3,256]{2,0,1:T(8,128)(2,1)} copy(bf16[128,3,256]{2,0,1:T(8,128)(2,1)S(1)} %bitcast.4) | data formatting | bytes 393216

commit v9 on v7

--- a/solution.py
+++ b/solution.py
@@ -474,13 +474,13 @@
     acc_ref[...] = gg_ref[...] * mix_ref[0]
     end_state(near, acc_ref, 1)
     send_x(1)
-    stage(1)
-    own_term()
-    combine_x(1)
     gg_ref[...] = gg_ref[...] * conv_ref[...]
     shift_copies(1, 0)
     shift_copies(1, 4)
     local_taps(1, 0, 8, acc_ref, True)
+    stage(1)
+    own_term()
+    combine_x(1)
     stage(2)
     local_taps(1, 8, 16, acc_ref, False)
     combine_z(1)

time: 57.8 us -> 57.8 us (level)
  no operation moved by 1% of the time
where the time goes in v9:
time: 57.8 us; the launch traced here: 57.7 us
  Pallas kernels  55.8 us (97%)
  local copies, waits for them, and re-layouts  1.33 us (2%)
  between operations  0.64 us (1%)
    pallas_call x1, Pallas kernels, per_device(): pl.pallas_call(kernel, out_shape=(jax.ShapeDtypeStruct((T, 2 * C), BF16),...  55.8 us
    unnamed x2, local copies, waits for them, and re-layouts  1.33 us

profile of v9, /device:TPU:1, one launch (start us, length us, event | category | flops | bytes accessed | tf_op | source)
XLA Modules:
  0.0 57.7 jit_solution(1960585701237063084)
XLA Ops:
  0.6 55.8 %shard_map.77 = (bf16[128,512]{1,0:T(8,128)(2,1)S(1)}, bf16[3,128,256]{2,1,0:T(8,128)(2,1)S(1)}) custom-call(bf16[3,128,256]{2,1,0:T(8,128)(2,1)} %bitcast.5, f32[3,3,256]{2,1,0:T(4,128)} %taps_in.1, f32[16,256]{1,0:T(8,128)} %bitcast.6, f32[16,256]{1,0:T(8,128)} %bitcast.7, bf16[256,256]{1,0:T(8,128)(2,1)} %w_ref.1, bf16[128,8192]{1,0:T(8,128)(2,1)} %go_ref.1), custom_call_target="tpu_custom_call" | custom-call | tf_op jit(solution)/shard_map/pallas_call | solution.py:533
  56.4 0.7 %copy.10 = bf16[128,512]{1,0:T(8,128)(2,1)} copy(bf16[128,512]{1,0:T(8,128)(2,1)S(1)} %get-tuple-element.8) | data formatting | bytes 262144
  57.1 0.7 %copy.11 = bf16[128,3,256]{2,0,1:T(8,128)(2,1)} copy(bf16[128,3,256]{2,0,1:T(8,128)(2,1)S(1)} %bitcast.4) | data formatting | bytes 393216
